TPU v7x, 32 devices: a whole 2x2x4 slice. The times are simulated.
32 devices in a mesh: slab: 2 (over x), shot: 8 (over z, y), rcv: 2 (over core).
Axes of the slice: x: 2, y: 2, z: 4, core: 2. Of those that a mesh axis runs over, the one named last changes fastest.
Arguments:
- traces: bfloat16 [16, 256, 1536], P(('slab', 'shot'), 'rcv'), parts along dimension 0, may hold values from -6 to 6
- rcv_delay: int32 [16, 256, 9], P(('slab', 'shot'), 'rcv'), parts along dimension 0, may hold values from 0 to 47
- rcv_frac: int32 [16, 256, 9], P(('slab', 'shot'), 'rcv'), parts along dimension 0, may hold values from 0 to 255
- live_count: int32 [16], P(('slab', 'shot')), parts along dimension 0, may hold values from 64 to 256
- src_delay: int32 [16, 2, 128, 9], P('slab', 'rcv', 'shot'), parts along dimension 0, may hold values from 0 to 47
- src_frac: int32 [16, 2, 128, 9], P('slab', 'rcv', 'shot'), parts along dimension 0, may hold values from 0 to 255
- rcv_taper: float32 [9], replicated, may hold values from 0.5 to 1.5
- src_taper: float32 [9], replicated, may hold values from 0.5 to 1.5
Outputs:
- redatumed: bfloat16 [16, 2, 128, 1536], P('slab', 'rcv', 'shot'), parts along dimension 0
There are 2 independent parts, one for each index of `slab`. A program takes and returns all parts, laid end to end along the dimension named above; an argument that names none is the same for every part. Nothing has to cross between parts.
All inputs are finite; a program needn't handle non-finite values.
Results may differ from a plain program's by a relative error of at most 0.0055.
Values may be sent and summed in bfloat16 or wider, within the bound.
No kernel may reach another device: no remote copies, remote signals or barrier semaphores. Data moves between devices by JAX's collectives and lax.ppermute only.
A program may use at most 64 MiB of HBM per device.

v0:
```python
import functools
import math

import jax
import jax.numpy as jnp
from jax import lax
from jax.experimental import pallas as pl
from jax.experimental.pallas import tpu as pltpu
from jax.sharding import PartitionSpec as P


AR = 4
AS = 4
TRI = 2
KR = 9
KS = 9
LANES = 128
SUB = 8
EDGE = 16
F32 = jnp.float32
BF16 = jnp.bfloat16
I32 = jnp.int32
GRANT = 24 << 20


def iota(shape, axis):
    return lax.broadcasted_iota(I32, shape, axis)


def filter_band(width):
    height = width + 2 * LANES
    away = jnp.abs(iota((height, width), 1) - (iota((height, width), 0) - LANES))
    energy = float(sum((TRI - abs(m)) ** 2 for m in range(1 - TRI, TRI)))
    return (jnp.maximum(TRI - away, 0).astype(F32) / math.sqrt(energy)).astype(BF16)


def pair_of(blocks):
    return 2 if blocks % 2 == 0 else 1


def filtered(source, band, store):
    blocks = source.shape[1] // LANES
    step = pair_of(blocks)
    for b in range(0, blocks, step):
        low, high = max(b - 1, 0), min(b + step + 1, blocks)
        start = (low - b + 1) * LANES
        part = source[:, low * LANES : high * LANES]
        dot = jnp.dot(part, band[start : start + (high - low) * LANES, :], preferred_element_type=F32)
        value = dot.astype(BF16).astype(F32)
        for i in range(step):
            store(b + i, value[:, i * LANES : (i + 1) * LANES])


def filtered_few(source, band):
    rows, time = source.shape
    blank = jnp.zeros((rows, LANES), BF16)
    wide = jnp.concatenate([blank, source, blank], axis=1)
    stack = jnp.concatenate([wide[:, t : t + 3 * LANES] for t in range(0, time, LANES)], axis=0)
    dot = jnp.dot(stack, band[: 3 * LANES, :LANES], preferred_element_type=F32).astype(BF16).astype(F32)
    return [dot[i : i + rows] for i in range(0, dot.shape[0], rows)]


def spread(table, pick):
    dims = (((0,), (0,)), ((), ()))
    return lax.dot_general(table.astype(F32).astype(BF16), pick.astype(BF16), dims, preferred_element_type=F32)


def weight_parts(frac, taper, keep):
    two = jnp.where(keep, frac * (taper * (1.0 / 256.0)), 0.0)
    one = jnp.where(keep, taper, 0.0) - two
    parts = []
    for value in (one, two):
        high = value.astype(BF16).astype(F32)
        parts += [high, value - high]
    return parts


def shifted(load, place, blocks):
    index = place & (LANES - 1)
    here = place < LANES
    moved = [jnp.take_along_axis(load(b), index, axis=1, mode="promise_in_bounds") for b in range(blocks)]
    moved.append(jnp.zeros_like(moved[0]))
    return [jnp.where(here, moved[b], moved[b + 1]) for b in range(blocks)]


def weighted(weights, taps, blocks, rows, lane):
    first, second = [], []
    step = pair_of(blocks)
    for b in range(0, blocks, step):
        stack = jnp.concatenate(
            [jnp.concatenate([tap[b + i] for tap in taps], axis=0).astype(BF16) for i in range(step)], axis=1
        )
        dot = jnp.dot(weights, stack, preferred_element_type=F32)
        for i in range(step):
            cols = slice(i * LANES, (i + 1) * LANES)
            first.append(dot[:rows, cols] + dot[rows : 2 * rows, cols])
            second.append(dot[2 * rows : 3 * rows, cols] + dot[3 * rows :, cols])
    rolled = [pltpu.roll(v, LANES - 1, 1) for v in second] + [jnp.zeros_like(second[0])]
    inner = lane < LANES - 1
    return [first[b] + jnp.where(inner, rolled[b], rolled[b + 1]) for b in range(blocks)]


def receiver_tables_kernel(
    live_in, taper_in, traces_in, delay_ref, frac_ref, place_ref, weight_ref, filt_ref, band_ref, live_ref, taper_ref, traces_ref, sem
):
    copies = [
        pltpu.make_async_copy(source, target, sem.at[i])
        for i, (source, target) in enumerate(((traces_in, traces_ref), (live_in, live_ref), (taper_in, taper_ref)))
    ]
    for copy in copies:
        copy.start()
    rows = delay_ref.shape[1]
    band_ref[...] = filter_band(band_ref.shape[1])
    for a in range(KR):
        pick = iota((KR, LANES), 0) == a
        place_ref[a] = iota((rows, LANES), 1) + spread(delay_ref[...], pick).astype(I32)
    wide = (rows, LANES)
    tap = iota((KR, LANES), 1) // SUB == iota((KR, LANES), 0)
    frac = spread(frac_ref[...], tap)
    row, lane = iota(wide, 0), iota(wide, 1)
    line = row + lax.axis_index("rcv") * rows
    copies[1].wait()
    copies[2].wait()
    live = jnp.minimum(live_ref[0], rows * lax.axis_size("rcv"))
    source = line + lane // SUB - AR
    keep = (lane % SUB == row % SUB) & (lane < KR * SUB) & (source >= 0) & (source < live)
    fold = jnp.minimum(line + AR, live - 1) - jnp.maximum(line - AR, 0) + 1
    taper = jnp.zeros(wide, F32)
    for a in range(KR):
        taper = jnp.where(lane // SUB == a, taper_ref[a], taper)
    taper = taper / jnp.sqrt(jnp.maximum(fold, 1).astype(F32))
    for i, part in enumerate(weight_parts(frac, taper, keep)):
        weight_ref[i] = part

    def store(b, value):
        filt_ref[b] = value

    copies[0].wait()
    filtered(traces_ref[...], band_ref, store)


def receiver_kernel(far, peers, other_ref, place_ref, weight_ref, filt_ref, band_ref, out_ref, src_ref):
    blocks, rows = filt_ref.shape[:2]
    part = rows // 2
    per_peer = rows // peers
    me = lax.axis_index("shot")
    mine = me // (peers // 2)
    half = (1 - mine) if far else mine
    low = me % (peers // 2)
    base = pl.multiple_of(half * part, part)

    left_at = pl.ds(pl.multiple_of(jnp.maximum(base - EDGE, 0), EDGE), EDGE)
    right_at = pl.ds(pl.multiple_of(jnp.minimum(base + part, rows - EDGE), EDGE), EDGE)
    far_side = pl.multiple_of(jnp.where(half == 0, rows - EDGE, 0), EDGE)
    other = filtered_few(other_ref[pl.ds(far_side, EDGE), :], band_ref)
    for b in range(blocks):
        src_ref[b, :EDGE] = jnp.where(half == 0, other[b], filt_ref[b, left_at, :])
        src_ref[b, EDGE : EDGE + part] = filt_ref[b, pl.ds(base, part), :]
        src_ref[b, EDGE + part :] = jnp.where(half == 1, other[b], filt_ref[b, right_at, :])

    lane = iota((SUB, LANES), 1)
    totals = []
    for g in range(part // SUB):
        at = pl.ds(pl.multiple_of(base + g * SUB, SUB), SUB)
        taps = []
        for a in range(KR):
            row = EDGE + g * SUB + a - AR
            taps.append(shifted(lambda b: src_ref[b, row : row + SUB, :], place_ref[a, at, :], blocks))
        weights = jnp.concatenate([weight_ref[i, at, : KR * SUB] for i in range(4)], axis=0).astype(BF16)
        totals.append(weighted(weights, taps, blocks, SUB, lane))
        step = max(1, min(2, per_peer // SUB))
        if len(totals) < step:
            continue
        first = (g + 1 - step) * SUB
        for s in range(0, step * SUB, min(step * SUB, per_peer)):
            height = min(step * SUB, per_peer)
            peer = ((first + s) // per_peer) ^ low
            start = (first + s) % per_peer
            for b in range(blocks):
                value = jnp.concatenate([t[b] for t in totals], axis=0).astype(BF16)
                out_ref[peer, start : start + height, b * LANES : (b + 1) * LANES] = value[s : s + height]
        totals = []


def source_tables_kernel(peers, taper_in, delay_ref, frac_ref, place_ref, weight_ref, taper_ref, sem):
    copy = pltpu.make_async_copy(taper_in, taper_ref, sem)
    copy.start()
    copy.wait()
    half_peers = peers // 2
    rows = delay_ref.shape[2]
    wide = half_peers * rows
    mine = lax.axis_index("shot") // half_peers
    for far in range(2):
        flip = mine == 1 - far
        sign = jnp.where(flip, -1, 1)
        for kk in range(peers):
            k = jnp.where(flip, peers - 1 - kk, kk)
            delay, frac = delay_ref[k], frac_ref[k]
            count = min(kk + AS, peers - 1) - max(kk - AS, 0) + 1
            row, lane = iota((rows, wide), 0), iota((rows, wide), 1)
            taper = jnp.zeros((rows, wide), F32)
            for pp in range(half_peers):
                if abs(pp - kk) <= AS:
                    tap = AS + sign * (pp - kk)
                    pick = iota((KS, LANES), 0) == tap
                    place_ref[far, kk, pp] = iota((rows, LANES), 1) + spread(delay, pick).astype(I32)
                    taper = jnp.where(lane // rows == pp, taper_ref[tap], taper)
            tap = AS + sign * (iota((KS, wide), 1) // rows - kk)
            keep = lane % rows == row
            parts = weight_parts(spread(frac, iota((KS, wide), 0) == tap), taper * (1.0 / math.sqrt(count)), keep)
            weight_ref[far, kk] = jnp.concatenate(parts, axis=0).astype(BF16)


def source_kernel(far, peers, place_ref, weight_ref, band_ref, *refs):
    half_peers = peers // 2
    ins = refs[:half_peers]
    refs = refs[half_peers:]
    if far:
        part_ref, out_ref, src_ref = refs
    else:
        out_ref, src_ref = refs
    per_peer, time = ins[0].shape
    blocks = time // LANES
    me = lax.axis_index("shot")
    mine = me // half_peers
    half = (1 - mine) if far else mine
    low = me % half_peers
    flip = half == 1
    slots = [jnp.where(flip, half_peers - 1 - (low ^ r), low ^ r) for r in range(half_peers)]

    def store(b, value):
        for r in range(half_peers):
            src_ref[slots[r], b] = value[r * per_peer : (r + 1) * per_peer]

    filtered(jnp.concatenate([ref[...] for ref in ins], axis=0), band_ref, store)
    rows = min(SUB, per_peer)
    lane = iota((per_peer, LANES), 1)
    for kk in range(peers):
        k = jnp.where(flip, peers - 1 - kk, kk)
        near = [pp for pp in range(half_peers) if abs(pp - kk) <= AS]
        if near:
            taps = []
            for pp in near:
                for i in range(0, per_peer, rows):
                    at = slice(i, i + rows)
                    taps.append(shifted(lambda b: src_ref[pp, b, at, :], place_ref[far, kk, pp, at, :], blocks))
            weights = weight_ref[far, kk, :, near[0] * per_peer : (near[-1] + 1) * per_peer]
            total = weighted(weights, taps, blocks, per_peer, lane)
        else:
            total = [jnp.zeros((per_peer, LANES), F32)] * blocks
        for b in range(blocks):
            cols = slice(b * LANES, (b + 1) * LANES)
            value = total[b]
            if far:
                value = value + part_ref[k, :, cols]
            out_ref[k, :, cols] = value.astype(out_ref.dtype)


VMEM = pl.BlockSpec(memory_space=pltpu.VMEM)
HBM = pl.BlockSpec(memory_space=pltpu.HBM)


def call(kernel, args, specs, outs, scratch=()):
    return pl.pallas_call(
        kernel,
        out_shape=outs,
        in_specs=specs,
        out_specs=[VMEM] * len(outs) if isinstance(outs, tuple) else VMEM,
        scratch_shapes=list(scratch),
        compiler_params=pltpu.CompilerParams(vmem_limit_bytes=GRANT),
    )(*args)


def body(traces, rcv_delay, rcv_frac, live_count, src_delay, src_frac, rcv_taper, src_taper):
    rows, time = traces.shape[1:]
    blocks = time // LANES
    peers = lax.axis_size("shot")
    half_peers = peers // 2
    per_peer = rows // peers
    traces = traces[0]
    other = lax.ppermute(traces, "rcv", [(0, 1), (1, 0)])
    shape = jax.ShapeDtypeStruct
    width = pair_of(blocks) * LANES

    place, weight, filt, band = call(
        receiver_tables_kernel,
        (live_count, rcv_taper, traces, rcv_delay[0].T, rcv_frac[0].T),
        [HBM, HBM, HBM, VMEM, VMEM],
        (
            shape((KR, rows, LANES), I32),
            shape((4, rows, LANES), F32),
            shape((blocks, rows, LANES), F32),
            shape((width + 2 * LANES, width), BF16),
        ),
        [
            pltpu.SMEM(live_count.shape, I32),
            pltpu.SMEM(rcv_taper.shape, F32),
            pltpu.VMEM(traces.shape, BF16),
            pltpu.SemaphoreType.DMA((3,)),
        ],
    )
    source_tables = call(
        functools.partial(source_tables_kernel, peers),
        (src_taper, *(jnp.transpose(v[:, 0], (0, 2, 1)) for v in (src_delay, src_frac))),
        [HBM, VMEM, VMEM],
        (
            shape((2, peers, half_peers, per_peer, LANES), I32),
            shape((2, peers, 4 * per_peer, half_peers * per_peer), BF16),
        ),
        [pltpu.SMEM(src_taper.shape, F32), pltpu.SemaphoreType.DMA],
    )

    def receivers(far):
        return call(
            functools.partial(receiver_kernel, far, peers),
            (other, place, weight, filt, band),
            [VMEM] * 5,
            shape((half_peers, per_peer, time), BF16),
            [pltpu.VMEM((blocks, rows // 2 + 2 * EDGE, LANES), F32)],
        )

    def sources(far, ins, partial=()):
        return call(
            functools.partial(source_kernel, far, peers),
            (*source_tables, band, *ins, *partial),
            [VMEM] * (3 + len(ins) + len(partial)),
            shape((peers, per_peer, time), BF16 if far else F32),
            [pltpu.VMEM((half_peers, blocks, per_peer, LANES), F32)],
        )

    far_out = receivers(1)
    far_in = [swap(far_out[r], r + half_peers, peers) for r in range(half_peers)]
    near_out = receivers(0)
    near_in = [near_out[0]] + [swap(near_out[r], r, peers) for r in range(1, half_peers)]
    partial = sources(0, near_in)
    result = sources(1, far_in, (partial,))
    return result.reshape(peers, 1, per_peer, time)


def swap(block, step, peers):
    return lax.ppermute(block, "shot", [(i, i ^ step) for i in range(peers)])


def solution(mesh):
    return jax.shard_map(
        body,
        mesh=mesh,
        in_specs=(
            P(("slab", "shot"), "rcv", None),
            P(("slab", "shot"), "rcv", None),
            P(("slab", "shot"), "rcv", None),
            P(("slab", "shot")),
            P("slab", "rcv", "shot", None),
            P("slab", "rcv", "shot", None),
            P(),
            P(),
        ),
        out_specs=P("slab", "rcv", "shot", None),
        check_vma=False,
    )
```

profile of v0, /device:TPU:0, one launch (start us, length us, event | category | flops | bytes accessed | tf_op | source)
XLA Modules:
  0.0 27.2 jit_solution(9691027581194833754)
XLA Ops:
  0.0 0.5 %collective-permute-start = (bf16[128,1536]{1,0:T(8,128)(2,1)}, bf16[128,1536]{1,0:T(8,128)(2,1)S(1)}, u32[]{:S(2)}, u32[]{:S(2)}) collective-permute-start(bf16[128,1536]{1,0:T(8,128)(2,1)} %bitcast.38), channel_id=1, source_target_pairs={{0,1},{1,0},{2,3},{3,2},{4,5},{5,4},{6,7},{7,6},{8,9},{9,8},{10,11... | collective-permute-start | bytes 1179656 | tf_op jit(solution)/shard_map/ppermute | solution.py:281
  1.1 0.7 %copy_bitcast_fusion.2 = (s32[9,128]{1,0:T(8,128)S(1)}, s32[9,128]{1,0:T(8,128)S(1)}) fusion(s32[1,128,9]{1,0,2:T(1,128)} %param.10, s32[1,128,9]{1,0,2:T(1,128)} %param.9), kind=kLoop, calls=%fused_computation.10 | loop fusion | bytes 18432 | tf_op jit(solution)/shard_map/transpose | solution.py:287
  1.9 0.0 copy-start.1
  1.9 0.7 %copy-done.1 = f32[9]{0:T(128)S(1)} copy-done((f32[9]{0:T(128)S(1)}, f32[9]{0:T(128)}, u32[]{:S(2)}) %copy-start.1) | copy-done | bytes 60
  2.5 0.0 copy-start
  2.5 1.0 %copy-done = bf16[1,128,1536]{2,1,0:T(8,128)(2,1)S(1)} copy-done((bf16[1,128,1536]{2,1,0:T(8,128)(2,1)S(1)}, bf16[1,128,1536]{2,1,0:T(8,128)(2,1)}, u32[]{:S(2)}) %copy-start) | copy-done | bytes 393240
  3.5 1.5 %shard_map.83 = (s32[9,128,128]{2,1,0:T(8,128)S(1)}, f32[4,128,128]{2,1,0:T(8,128)S(1)}, f32[12,128,128]{2,1,0:T(8,128)S(1)}, bf16[512,256]{1,0:T(8,128)(2,1)S(1)}) custom-call(s32[1]{0:T(128)S(6)} %copy.23.live_in, f32[9]{0:T(128)S(1)} %copy-done.1, bf16[128,1536]{1,0:T(8,128)(2,1)S(1)} %bitcast.39, s32[9,128]{1,0:T(8,128)S(1)} %get-tuple-element.28.delay_ref, ...), custom_call_target="tpu_custom_call" | custom-call | tf_op jit(solution)/shard_map/pallas_call | solution.py:264
  5.0 0.0 collective-permute-done.other_ref
  5.1 1.5 %shard_map.85 = bf16[4,16,1536]{2,1,0:T(8,128)(2,1)S(1)} custom-call(bf16[128,1536]{1,0:T(8,128)(2,1)S(1)} %collective-permute-done.other_ref, s32[9,128,128]{2,1,0:T(8,128)S(1)} %get-tuple-element.14.place_ref, f32[4,128,128]{2,1,0:T(8,128)S(1)} %get-tuple-element.15.weight_ref, f32[12,128,128]{2,1,0:T(8,128)S(1)} %get-tuple-element.16.filt_ref, ...), custom_call_target="tpu_custom_call" | custom-call | tf_op jit(solution)/shard_map/pallas_call | solution.py:264
  6.6 3.6 %collective-permute-start.7 = (bf16[16,1536]{1,0:T(8,128)(2,1)S(1)}, bf16[16,1536]{1,0:T(8,128)(2,1)S(1)}, u32[]{:S(2)}, u32[]{:S(2)}) collective-permute-start(bf16[16,1536]{1,0:T(8,128)(2,1)S(1)} %get-tuple-element.17), channel_id=1, source_target_pairs={{0,6},{2,4},{4,2},{6,0},{8,14},{10,12},{12,10},{14,8},{1,7},{3,5},... | collective-permute-start | bytes 147464 | tf_op jit(solution)/shard_map/ppermute | solution.py:341
  10.2 0.4 %collective-permute-start.6 = (bf16[16,1536]{1,0:T(8,128)(2,1)S(1)}, bf16[16,1536]{1,0:T(8,128)(2,1)S(1)}, u32[]{:S(2)}, u32[]{:S(2)}) collective-permute-start(bf16[16,1536]{1,0:T(8,128)(2,1)S(1)} %get-tuple-element.18), channel_id=1, source_target_pairs={{0,4},{2,6},{4,0},{6,2},{8,12},{10,14},{12,8},{14,10},{1,5},{3,7},... | collective-permute-start | bytes 147464 | tf_op jit(solution)/shard_map/ppermute | solution.py:341
  10.6 1.5 %shard_map.84 = bf16[4,16,1536]{2,1,0:T(8,128)(2,1)S(1)} custom-call(bf16[128,1536]{1,0:T(8,128)(2,1)S(1)} %collective-permute-done.other_ref, s32[9,128,128]{2,1,0:T(8,128)S(1)} %get-tuple-element.14.place_ref, f32[4,128,128]{2,1,0:T(8,128)S(1)} %get-tuple-element.15.weight_ref, f32[12,128,128]{2,1,0:T(8,128)S(1)} %get-tuple-element.16.filt_ref, ...), custom_call_target="tpu_custom_call" | custom-call | tf_op jit(solution)/shard_map/pallas_call | solution.py:264
  12.1 0.0 copy-start.3
  12.1 0.0 copy-start.4
  12.1 0.3 collective-permute-start.5
  12.4 4.9 %collective-permute-start.4 = (bf16[16,1536]{1,0:T(8,128)(2,1)S(1)}, bf16[16,1536]{1,0:T(8,128)(2,1)S(1)}, u32[]{:S(2)}, u32[]{:S(2)}) collective-permute-start(bf16[16,1536]{1,0:T(8,128)(2,1)S(1)} %get-tuple-element.21), channel_id=1, source_target_pairs={{0,14},{2,12},{4,10},{6,8},{8,6},{10,4},{12,2},{14,0},{1,15},{3,13... | collective-permute-start | bytes 147464 | tf_op jit(solution)/shard_map/ppermute | solution.py:341
  17.3 0.2 collective-permute-start.3
  17.5 0.0 collective-permute-done.7.refs_3_
  17.5 0.7 %collective-permute-start.2 = (bf16[16,1536]{1,0:T(8,128)(2,1)S(1)}, bf16[16,1536]{1,0:T(8,128)(2,1)S(1)}, u32[]{:S(2)}, u32[]{:S(2)}) collective-permute-start(bf16[16,1536]{1,0:T(8,128)(2,1)S(1)} %get-tuple-element.23), channel_id=1, source_target_pairs={{0,10},{2,8},{4,14},{6,12},{8,2},{10,0},{12,6},{14,4},{1,11},{3,9}... | collective-permute-start | bytes 147464 | tf_op jit(solution)/shard_map/ppermute | solution.py:341
  18.2 0.0 collective-permute-done.6.refs_2_
  18.2 2.0 %collective-permute-start.1 = (bf16[16,1536]{1,0:T(8,128)(2,1)S(1)}, bf16[16,1536]{1,0:T(8,128)(2,1)S(1)}, u32[]{:S(2)}, u32[]{:S(2)}) collective-permute-start(bf16[16,1536]{1,0:T(8,128)(2,1)S(1)} %get-tuple-element.24), channel_id=1, source_target_pairs={{0,8},{2,10},{4,12},{6,14},{8,0},{10,2},{12,4},{14,6},{1,9},{3,11}... | collective-permute-start | bytes 147464 | tf_op jit(solution)/shard_map/ppermute | solution.py:341
  20.2 0.0 copy-done.3
  20.2 0.0 copy-done.4
  20.2 0.0 copy-start.2
  20.2 0.6 %copy-done.2 = f32[9]{0:T(128)S(1)} copy-done((f32[9]{0:T(128)S(1)}, f32[9]{0:T(128)}, u32[]{:S(2)}) %copy-start.2) | copy-done | bytes 60
  20.9 0.9 %shard_map.82 = (s32[2,8,4,16,128]{4,3,2,1,0:T(8,128)S(1)}, bf16[2,8,64,64]{3,2,1,0:T(8,128)(2,1)S(1)}) custom-call(f32[9]{0:T(128)S(1)} %copy-done.2, s32[8,9,16]{2,1,0:T(8,128)S(1)} %get-tuple-element.26.delay_ref, s32[8,9,16]{2,1,0:T(8,128)S(1)} %get-tuple-element.25.frac_ref), custom_call_target="tpu_custom_call" | custom-call | tf_op jit(solution)/shard_map/pallas_call | solution.py:264
  21.8 0.0 collective-permute-done.5.refs_1_
  21.8 1.3 %shard_map.86.refs_4_ = f32[8,16,1536]{2,1,0:T(8,128)S(1)} custom-call(s32[2,8,4,16,128]{4,3,2,1,0:T(8,128)S(1)} %get-tuple-element.11.place_ref, bf16[2,8,64,64]{3,2,1,0:T(8,128)(2,1)S(1)} %get-tuple-element.12.weight_ref, bf16[512,256]{1,0:T(8,128)(2,1)S(1)} %get-tuple-element.13.band_ref, bf16[16,1536]{1,0:T(8,128)(2,1)S(1)} %get-tuple-element.20.refs_0_, ...), custom_call_target="tpu_custom_call" | custom-call | tf_op jit(solution)/shard_map/pallas_call | solution.py:264
  23.1 0.0 collective-permute-done.4.refs_3_
  23.1 0.1 collective-permute-done.3.refs_2_
  23.2 2.0 %collective-permute-done.2.refs_1_ = bf16[16,1536]{1,0:T(8,128)(2,1)S(1)} collective-permute-done((bf16[16,1536]{1,0:T(8,128)(2,1)S(1)}, bf16[16,1536]{1,0:T(8,128)(2,1)S(1)}, u32[]{:S(2)}, u32[]{:S(2)}) %collective-permute-start.2) | collective-permute-done | bytes 49184 | tf_op jit(solution)/shard_map/ppermute | solution.py:341
  25.2 0.0 collective-permute-done.1.refs_0_
  25.2 2.0 %shard_map.87 = bf16[8,16,1536]{2,1,0:T(8,128)(2,1)} custom-call(s32[2,8,4,16,128]{4,3,2,1,0:T(8,128)S(1)} %get-tuple-element.11.place_ref, bf16[2,8,64,64]{3,2,1,0:T(8,128)(2,1)S(1)} %get-tuple-element.12.weight_ref, bf16[512,256]{1,0:T(8,128)(2,1)S(1)} %get-tuple-element.13.band_ref, bf16[16,1536]{1,0:T(8,128)(2,1)S(1)} %collective-permute-done.1.refs_0_, ...), custom_call_target="tpu_custom_call" | custom-call | tf_op jit(solution)/shard_map/pallas_call | solution.py:264
  (3 shorter events, 0.0 us)
Async XLA Ops:
  0.0 5.0 %collective-permute-start = (bf16[128,1536]{1,0:T(8,128)(2,1)}, bf16[128,1536]{1,0:T(8,128)(2,1)S(1)}, u32[]{:S(2)}, u32[]{:S(2)}) collective-permute-start(bf16[128,1536]{1,0:T(8,128)(2,1)} %bitcast.38), channel_id=1, source_target_pairs={{0,1},{1,0},{2,3},{3,2},{4,5},{5,4},{6,7},{7,6},{8,9},{9,8},{10,11... | collective-permute-start | bytes 1179656 | tf_op jit(solution)/shard_map/ppermute | solution.py:281
  1.9 0.7 %copy-start.1 = (f32[9]{0:T(128)S(1)}, f32[9]{0:T(128)}, u32[]{:S(2)}) copy-start(f32[9]{0:T(128)} %taper_in.3) | copy-start | bytes 112
  2.5 1.0 %copy-start = (bf16[1,128,1536]{2,1,0:T(8,128)(2,1)S(1)}, bf16[1,128,1536]{2,1,0:T(8,128)(2,1)}, u32[]{:S(2)}) copy-start(bf16[1,128,1536]{2,1,0:T(8,128)(2,1)} %param.8) | copy-start | bytes 1179652
  6.6 10.9 %collective-permute-start.7 = (bf16[16,1536]{1,0:T(8,128)(2,1)S(1)}, bf16[16,1536]{1,0:T(8,128)(2,1)S(1)}, u32[]{:S(2)}, u32[]{:S(2)}) collective-permute-start(bf16[16,1536]{1,0:T(8,128)(2,1)S(1)} %get-tuple-element.17), channel_id=1, source_target_pairs={{0,6},{2,4},{4,2},{6,0},{8,14},{10,12},{12,10},{14,8},{1,7},{3,5},... | collective-permute-start | bytes 147464 | tf_op jit(solution)/shard_map/ppermute | solution.py:341
  10.2 8.1 %collective-permute-start.6 = (bf16[16,1536]{1,0:T(8,128)(2,1)S(1)}, bf16[16,1536]{1,0:T(8,128)(2,1)S(1)}, u32[]{:S(2)}, u32[]{:S(2)}) collective-permute-start(bf16[16,1536]{1,0:T(8,128)(2,1)S(1)} %get-tuple-element.18), channel_id=1, source_target_pairs={{0,4},{2,6},{4,0},{6,2},{8,12},{10,14},{12,8},{14,10},{1,5},{3,7},... | collective-permute-start | bytes 147464 | tf_op jit(solution)/shard_map/ppermute | solution.py:341
  12.1 8.1 %copy-start.3 = (s32[8,1,16,9]{2,1,3,0:T(1,128)S(1)}, s32[8,1,16,9]{2,1,3,0:T(1,128)}, u32[]{:S(2)}) copy-start(s32[8,1,16,9]{2,1,3,0:T(1,128)} %param.13) | copy-start | bytes 13828
  12.1 8.1 %copy-start.4 = (s32[8,1,16,9]{2,1,3,0:T(1,128)S(1)}, s32[8,1,16,9]{2,1,3,0:T(1,128)}, u32[]{:S(2)}) copy-start(s32[8,1,16,9]{2,1,3,0:T(1,128)} %param.12) | copy-start | bytes 13828
  12.1 9.7 %collective-permute-start.5 = (bf16[16,1536]{1,0:T(8,128)(2,1)S(1)}, bf16[16,1536]{1,0:T(8,128)(2,1)S(1)}, u32[]{:S(2)}, u32[]{:S(2)}) collective-permute-start(bf16[16,1536]{1,0:T(8,128)(2,1)S(1)} %get-tuple-element.19), channel_id=1, source_target_pairs={{0,2},{2,0},{4,6},{6,4},{8,10},{10,8},{12,14},{14,12},{1,3},{3,1},... | collective-permute-start | bytes 147464 | tf_op jit(solution)/shard_map/ppermute | solution.py:341
  12.4 10.7 %collective-permute-start.4 = (bf16[16,1536]{1,0:T(8,128)(2,1)S(1)}, bf16[16,1536]{1,0:T(8,128)(2,1)S(1)}, u32[]{:S(2)}, u32[]{:S(2)}) collective-permute-start(bf16[16,1536]{1,0:T(8,128)(2,1)S(1)} %get-tuple-element.21), channel_id=1, source_target_pairs={{0,14},{2,12},{4,10},{6,8},{8,6},{10,4},{12,2},{14,0},{1,15},{3,13... | collective-permute-start | bytes 147464 | tf_op jit(solution)/shard_map/ppermute | solution.py:341
  17.3 5.9 %collective-permute-start.3 = (bf16[16,1536]{1,0:T(8,128)(2,1)S(1)}, bf16[16,1536]{1,0:T(8,128)(2,1)S(1)}, u32[]{:S(2)}, u32[]{:S(2)}) collective-permute-start(bf16[16,1536]{1,0:T(8,128)(2,1)S(1)} %get-tuple-element.22), channel_id=1, source_target_pairs={{0,12},{2,14},{4,8},{6,10},{8,4},{10,6},{12,0},{14,2},{1,13},{3,15... | collective-permute-start | bytes 147464 | tf_op jit(solution)/shard_map/ppermute | solution.py:341
  17.5 7.7 %collective-permute-start.2 = (bf16[16,1536]{1,0:T(8,128)(2,1)S(1)}, bf16[16,1536]{1,0:T(8,128)(2,1)S(1)}, u32[]{:S(2)}, u32[]{:S(2)}) collective-permute-start(bf16[16,1536]{1,0:T(8,128)(2,1)S(1)} %get-tuple-element.23), channel_id=1, source_target_pairs={{0,10},{2,8},{4,14},{6,12},{8,2},{10,0},{12,6},{14,4},{1,11},{3,9}... | collective-permute-start | bytes 147464 | tf_op jit(solution)/shard_map/ppermute | solution.py:341
  18.2 7.0 %collective-permute-start.1 = (bf16[16,1536]{1,0:T(8,128)(2,1)S(1)}, bf16[16,1536]{1,0:T(8,128)(2,1)S(1)}, u32[]{:S(2)}, u32[]{:S(2)}) collective-permute-start(bf16[16,1536]{1,0:T(8,128)(2,1)S(1)} %get-tuple-element.24), channel_id=1, source_target_pairs={{0,8},{2,10},{4,12},{6,14},{8,0},{10,2},{12,4},{14,6},{1,9},{3,11}... | collective-permute-start | bytes 147464 | tf_op jit(solution)/shard_map/ppermute | solution.py:341
  20.2 0.7 %copy-start.2 = (f32[9]{0:T(128)S(1)}, f32[9]{0:T(128)}, u32[]{:S(2)}) copy-start(f32[9]{0:T(128)} %taper_in.2) | copy-start | bytes 112
where the time goes:
time: 27.5 us; the launch traced here: 27.2 us
  starting transfers between devices  12.6 us (46%)
  Pallas kernels  8.73 us (32%)
  local copies, waits for them, and re-layouts  3.06 us (11%)
  waiting for transfers between devices  2.13 us (8%)
  between operations  0.74 us (3%)
    ppermute x7, starting transfers between devices, swap(): return lax.ppermute(block, 'shot', [(i, i ^ step) for i in range(peers)])  12.1 us
    pallas_call x6, Pallas kernels, call(): pl.pallas_call(kernel, out_shape=outs, in_specs=specs, out_specs=[VMEM] *...  8.73 us
    unnamed x10, local copies, waits for them, and re-layouts  2.31 us
    ppermute x7, waiting for transfers between devices, swap(): return lax.ppermute(block, 'shot', [(i, i ^ step) for i in range(peers)])  2.13 us
    transpose x1, local copies, waits for them, and re-layouts, body(): rcv_frac[0]  0.71 us
  transfers between devices with their start and end apart: 8, of which 2 were waited for; matrix products, arithmetic and copies ran while one was open for 3% of the time, Pallas kernels for 19%

commit v1 on v0

--- a/solution.py
+++ b/solution.py
@@ -21,6 +21,9 @@
 BF16 = jnp.bfloat16
 I32 = jnp.int32
 GRANT = 24 << 20
+LIVE = 2 * KR
+TAPER = LIVE + 1
+SOURCE_TAPER = TAPER + 1
 
 
 def iota(shape, axis):
@@ -100,42 +103,36 @@
     return [first[b] + jnp.where(inner, rolled[b], rolled[b + 1]) for b in range(blocks)]
 
 
-def receiver_tables_kernel(
-    live_in, taper_in, traces_in, delay_ref, frac_ref, place_ref, weight_ref, filt_ref, band_ref, live_ref, taper_ref, traces_ref, sem
-):
-    copies = [
-        pltpu.make_async_copy(source, target, sem.at[i])
-        for i, (source, target) in enumerate(((traces_in, traces_ref), (live_in, live_ref), (taper_in, taper_ref)))
-    ]
-    for copy in copies:
-        copy.start()
-    rows = delay_ref.shape[1]
+def lookup(row, index):
+    wide = jnp.broadcast_to(row, (SUB, LANES))
+    return jnp.take_along_axis(wide, index[:SUB], axis=1, mode="promise_in_bounds")[:1]
+
+
+def receiver_tables_kernel(small_ref, place_ref, weight_ref, band_ref):
+    rows = small_ref.shape[1]
+    delay, frac = small_ref[:KR, :], small_ref[KR : 2 * KR, :]
     band_ref[...] = filter_band(band_ref.shape[1])
     for a in range(KR):
         pick = iota((KR, LANES), 0) == a
-        place_ref[a] = iota((rows, LANES), 1) + spread(delay_ref[...], pick).astype(I32)
+        place_ref[a] = iota((rows, LANES), 1) + spread(delay, pick).astype(I32)
     wide = (rows, LANES)
     tap = iota((KR, LANES), 1) // SUB == iota((KR, LANES), 0)
-    frac = spread(frac_ref[...], tap)
     row, lane = iota(wide, 0), iota(wide, 1)
     line = row + lax.axis_index("rcv") * rows
-    copies[1].wait()
-    copies[2].wait()
-    live = jnp.minimum(live_ref[0], rows * lax.axis_size("rcv"))
+    live = jnp.minimum(small_ref[LIVE : LIVE + 1, :LANES].astype(I32), rows * lax.axis_size("rcv"))
     source = line + lane // SUB - AR
     keep = (lane % SUB == row % SUB) & (lane < KR * SUB) & (source >= 0) & (source < live)
     fold = jnp.minimum(line + AR, live - 1) - jnp.maximum(line - AR, 0) + 1
-    taper = jnp.zeros(wide, F32)
-    for a in range(KR):
-        taper = jnp.where(lane // SUB == a, taper_ref[a], taper)
+    taper = lookup(small_ref[TAPER : TAPER + 1, :LANES], lane // SUB)
     taper = taper / jnp.sqrt(jnp.maximum(fold, 1).astype(F32))
-    for i, part in enumerate(weight_parts(frac, taper, keep)):
+    for i, part in enumerate(weight_parts(spread(frac, tap), taper, keep)):
         weight_ref[i] = part
 
+
+def filter_kernel(traces_ref, band_ref, filt_ref):
     def store(b, value):
         filt_ref[b] = value
 
-    copies[0].wait()
     filtered(traces_ref[...], band_ref, store)
 
 
@@ -182,92 +179,85 @@
         totals = []
 
 
-def source_tables_kernel(peers, taper_in, delay_ref, frac_ref, place_ref, weight_ref, taper_ref, sem):
-    copy = pltpu.make_async_copy(taper_in, taper_ref, sem)
-    copy.start()
-    copy.wait()
-    half_peers = peers // 2
-    rows = delay_ref.shape[2]
-    wide = half_peers * rows
-    mine = lax.axis_index("shot") // half_peers
-    for far in range(2):
-        flip = mine == 1 - far
-        sign = jnp.where(flip, -1, 1)
-        for kk in range(peers):
-            k = jnp.where(flip, peers - 1 - kk, kk)
-            delay, frac = delay_ref[k], frac_ref[k]
-            count = min(kk + AS, peers - 1) - max(kk - AS, 0) + 1
-            row, lane = iota((rows, wide), 0), iota((rows, wide), 1)
-            taper = jnp.zeros((rows, wide), F32)
-            for pp in range(half_peers):
-                if abs(pp - kk) <= AS:
-                    tap = AS + sign * (pp - kk)
-                    pick = iota((KS, LANES), 0) == tap
-                    place_ref[far, kk, pp] = iota((rows, LANES), 1) + spread(delay, pick).astype(I32)
-                    taper = jnp.where(lane // rows == pp, taper_ref[tap], taper)
-            tap = AS + sign * (iota((KS, wide), 1) // rows - kk)
-            keep = lane % rows == row
-            parts = weight_parts(spread(frac, iota((KS, wide), 0) == tap), taper * (1.0 / math.sqrt(count)), keep)
-            weight_ref[far, kk] = jnp.concatenate(parts, axis=0).astype(BF16)
-
-
-def source_kernel(far, peers, place_ref, weight_ref, band_ref, *refs):
-    half_peers = peers // 2
-    ins = refs[:half_peers]
-    refs = refs[half_peers:]
-    if far:
-        part_ref, out_ref, src_ref = refs
+def source_tables_kernel(peers, share, small_ref, table_ref, place_ref, weight_ref):
+    rows = table_ref.shape[2]
+    wide = share * rows
+    for k in range(peers):
+        delay, frac = table_ref[k, :KS], table_ref[k, KS:]
+        count = min(k + AS, peers - 1) - max(k - AS, 0) + 1
+        for p in range(peers):
+            place = iota((rows, LANES), 1)
+            if abs(p - k) <= AS:
+                place = place + spread(delay, iota((KS, LANES), 0) == p - k + AS).astype(I32)
+            place_ref[k, p] = place
+        row, lane = iota((rows, LANES), 0), iota((rows, LANES), 1)
+        for q in range(peers // share):
+            tap = AS + q * share + lane // rows - k
+            keep = (lane % rows == row) & (tap >= 0) & (tap < KS) & (lane < wide)
+            index = jnp.clip(AS + q * share + iota((SUB, LANES), 1) // rows - k, 0, KS - 1)
+            taper = lookup(small_ref[SOURCE_TAPER : SOURCE_TAPER + 1, :LANES], index) * (1.0 / math.sqrt(count))
+            column = AS + q * share + iota((KS, LANES), 1) // rows - k
+            parts = weight_parts(spread(frac, column == iota((KS, LANES), 0)), taper, keep)
+            weight_ref[k, q] = jnp.concatenate(parts, axis=0).astype(BF16)[:, :wide]
+
+
+def source_kernel(call_index, last, peers, share, place_ref, weight_ref, band_ref, *refs):
+    ins, refs = refs[:share], refs[share:]
+    if call_index:
+        part_ref, refs = refs[0], refs[1:]
+    if last:
+        out_ref, src_ref, done_ref, sem = refs
     else:
         out_ref, src_ref = refs
     per_peer, time = ins[0].shape
     blocks = time // LANES
     me = lax.axis_index("shot")
-    mine = me // half_peers
-    half = (1 - mine) if far else mine
-    low = me % half_peers
-    flip = half == 1
-    slots = [jnp.where(flip, half_peers - 1 - (low ^ r), low ^ r) for r in range(half_peers)]
+    group = (me // share) ^ call_index
+    slots = [(me % share) ^ i for i in range(share)]
 
     def store(b, value):
-        for r in range(half_peers):
-            src_ref[slots[r], b] = value[r * per_peer : (r + 1) * per_peer]
+        for i in range(share):
+            src_ref[slots[i], b] = value[i * per_peer : (i + 1) * per_peer]
 
     filtered(jnp.concatenate([ref[...] for ref in ins], axis=0), band_ref, store)
     rows = min(SUB, per_peer)
     lane = iota((per_peer, LANES), 1)
-    for kk in range(peers):
-        k = jnp.where(flip, peers - 1 - kk, kk)
-        near = [pp for pp in range(half_peers) if abs(pp - kk) <= AS]
-        if near:
-            taps = []
-            for pp in near:
-                for i in range(0, per_peer, rows):
-                    at = slice(i, i + rows)
-                    taps.append(shifted(lambda b: src_ref[pp, b, at, :], place_ref[far, kk, pp, at, :], blocks))
-            weights = weight_ref[far, kk, :, near[0] * per_peer : (near[-1] + 1) * per_peer]
-            total = weighted(weights, taps, blocks, per_peer, lane)
-        else:
-            total = [jnp.zeros((per_peer, LANES), F32)] * blocks
+    copies = []
+    for k in range(peers):
+        taps = []
+        for e in range(share):
+            for i in range(0, per_peer, rows):
+                at = slice(i, i + rows)
+                place = place_ref[k, group * share + e, at, :]
+                taps.append(shifted(lambda b: src_ref[e, b, at, :], place, blocks))
+        total = weighted(weight_ref[k, group], taps, blocks, per_peer, lane)
+        target = done_ref if last else out_ref
         for b in range(blocks):
             cols = slice(b * LANES, (b + 1) * LANES)
             value = total[b]
-            if far:
+            if call_index:
                 value = value + part_ref[k, :, cols]
-            out_ref[k, :, cols] = value.astype(out_ref.dtype)
+            target[k, :, cols] = value.astype(target.dtype)
+        if last:
+            copies.append(pltpu.make_async_copy(done_ref.at[k], out_ref.at[k], sem.at[k]))
+            copies[-1].start()
+    for copy in copies:
+        copy.wait()
 
 
 VMEM = pl.BlockSpec(memory_space=pltpu.VMEM)
-HBM = pl.BlockSpec(memory_space=pltpu.HBM)
-
-
-def call(kernel, args, specs, outs, scratch=()):
+ANY = pl.BlockSpec(memory_space=pl.ANY)
+
+
+def call(kernel, args, outs, scratch=(), cost=0, out_specs=None):
     return pl.pallas_call(
         kernel,
         out_shape=outs,
-        in_specs=specs,
-        out_specs=[VMEM] * len(outs) if isinstance(outs, tuple) else VMEM,
+        in_specs=[VMEM] * len(args),
+        out_specs=out_specs or ([VMEM] * len(outs) if isinstance(outs, tuple) else VMEM),
         scratch_shapes=list(scratch),
         compiler_params=pltpu.CompilerParams(vmem_limit_bytes=GRANT),
+        cost_estimate=pl.CostEstimate(flops=cost, bytes_accessed=0, transcendentals=0) if cost else None,
     )(*args)
 
 
@@ -282,58 +272,68 @@
     shape = jax.ShapeDtypeStruct
     width = pair_of(blocks) * LANES
 
-    place, weight, filt, band = call(
+    share = max(1, peers // 4)
+    lanes = max(rows, LANES)
+    small = jnp.concatenate(
+        [
+            jnp.pad(rcv_delay[0].T.astype(F32), ((0, 0), (0, lanes - rows))),
+            jnp.pad(rcv_frac[0].T.astype(F32), ((0, 0), (0, lanes - rows))),
+            jnp.broadcast_to(live_count.astype(F32)[:, None], (1, lanes)),
+            jnp.pad(rcv_taper[None], ((0, 0), (0, lanes - KR))),
+            jnp.pad(src_taper[None], ((0, 0), (0, lanes - KS))),
+        ],
+        axis=0,
+    )
+    place, weight, band = call(
         receiver_tables_kernel,
-        (live_count, rcv_taper, traces, rcv_delay[0].T, rcv_frac[0].T),
-        [HBM, HBM, HBM, VMEM, VMEM],
+        (small,),
         (
             shape((KR, rows, LANES), I32),
             shape((4, rows, LANES), F32),
-            shape((blocks, rows, LANES), F32),
             shape((width + 2 * LANES, width), BF16),
         ),
-        [
-            pltpu.SMEM(live_count.shape, I32),
-            pltpu.SMEM(rcv_taper.shape, F32),
-            pltpu.VMEM(traces.shape, BF16),
-            pltpu.SemaphoreType.DMA((3,)),
-        ],
+        cost=2_000_000_000,
     )
-    source_tables = call(
-        functools.partial(source_tables_kernel, peers),
-        (src_taper, *(jnp.transpose(v[:, 0], (0, 2, 1)) for v in (src_delay, src_frac))),
-        [HBM, VMEM, VMEM],
-        (
-            shape((2, peers, half_peers, per_peer, LANES), I32),
-            shape((2, peers, 4 * per_peer, half_peers * per_peer), BF16),
-        ),
-        [pltpu.SMEM(src_taper.shape, F32), pltpu.SemaphoreType.DMA],
-    )
+    filt = call(filter_kernel, (traces, band), shape((blocks, rows, LANES), F32))
 
     def receivers(far):
         return call(
             functools.partial(receiver_kernel, far, peers),
             (other, place, weight, filt, band),
-            [VMEM] * 5,
             shape((half_peers, per_peer, time), BF16),
             [pltpu.VMEM((blocks, rows // 2 + 2 * EDGE, LANES), F32)],
-        )
-
-    def sources(far, ins, partial=()):
-        return call(
-            functools.partial(source_kernel, far, peers),
-            (*source_tables, band, *ins, *partial),
-            [VMEM] * (3 + len(ins) + len(partial)),
-            shape((peers, per_peer, time), BF16 if far else F32),
-            [pltpu.VMEM((half_peers, blocks, per_peer, LANES), F32)],
         )
 
     far_out = receivers(1)
     far_in = [swap(far_out[r], r + half_peers, peers) for r in range(half_peers)]
     near_out = receivers(0)
     near_in = [near_out[0]] + [swap(near_out[r], r, peers) for r in range(1, half_peers)]
-    partial = sources(0, near_in)
-    result = sources(1, far_in, (partial,))
+
+    table = jnp.concatenate([jnp.transpose(v[:, 0], (0, 2, 1)).astype(F32) for v in (src_delay, src_frac)], axis=1)
+    source_tables = call(
+        functools.partial(source_tables_kernel, peers, share),
+        (small, table),
+        (
+            shape((peers, peers, per_peer, LANES), I32),
+            shape((peers, peers // share, 4 * per_peer, share * per_peer), BF16),
+        ),
+    )
+    arrived = near_in + far_in
+    result = None
+    turns = range(peers // share)
+    for turn in turns:
+        last = turn == turns[-1]
+        extra = [] if turn == 0 else [result]
+        scratch = [pltpu.VMEM((share, blocks, per_peer, LANES), F32)]
+        if last:
+            scratch += [pltpu.VMEM((peers, per_peer, time), BF16), pltpu.SemaphoreType.DMA((peers,))]
+        result = call(
+            functools.partial(source_kernel, turn, last, peers, share),
+            (*source_tables, band, *arrived[turn * share : (turn + 1) * share], *extra),
+            shape((peers, per_peer, time), BF16 if last else F32),
+            scratch,
+            out_specs=ANY if last else VMEM,
+        )
     return result.reshape(peers, 1, per_peer, time)
 
 

time: 27.5 us -> 26.9 us (0.978)
  local copies, waits for them, and re-layouts: 3.06 us -> 1.77 us
  Pallas kernels: 8.73 us -> 9.59 us
  waiting for transfers between devices: 2.13 us -> 1.76 us
    pallas_call x6 -> x9, Pallas kernels: 8.73 us -> 9.59 us  [call(): pl.pallas_call(kernel, out_shape=outs, in_specs=[VMEM] * len(args), out_s...]
    transpose x2 -> x0, local copies, waits for them, and re-layouts: 0.72 us -> none  [the longest x1 0.71 us: body(): rcv_frac[0]]
    unnamed x10 -> x14, local copies, waits for them, and re-layouts: 2.31 us -> 1.59 us
    ppermute x7, waiting for transfers between devices: 2.13 us -> 1.76 us  [swap(): return lax.ppermute(block, 'shot', [(i, i ^ step) for i in range(peers)])]
  transfers between devices with their start and end apart: 8 -> 8, of which waited for: 2 -> 2; matrix products, arithmetic and copies ran while one was open for 3% -> 1% of each run, Pallas kernels for 19% -> 23%
where the time goes in v1:
time: 26.9 us; the launch traced here: 26.6 us
  starting transfers between devices  12.7 us (47%)
  Pallas kernels  9.59 us (36%)
  local copies, waits for them, and re-layouts  1.77 us (7%)
  waiting for transfers between devices  1.76 us (7%)
  between operations  0.84 us (3%)
    ppermute x7, starting transfers between devices, swap(): return lax.ppermute(block, 'shot', [(i, i ^ step) for i in range(peers)])  12.2 us
    pallas_call x9, Pallas kernels, call(): pl.pallas_call(kernel, out_shape=outs, in_specs=[VMEM] * len(args), out_s...  9.59 us
    ppermute x7, waiting for transfers between devices, swap(): return lax.ppermute(block, 'shot', [(i, i ^ step) for i in range(peers)])  1.76 us
    unnamed x14, local copies, waits for them, and re-layouts  1.59 us
  transfers between devices with their start and end apart: 8, of which 2 were waited for; matrix products, arithmetic and copies ran while one was open for 1% of the time, Pallas kernels for 23%

profile of v1, /device:TPU:0, one launch (start us, length us, event | category | flops | bytes accessed | tf_op | source)
XLA Modules:
  0.0 26.6 jit_solution(8714851450499977591)
XLA Ops:
  0.0 0.5 %collective-permute-start = (bf16[128,1536]{1,0:T(8,128)(2,1)}, bf16[128,1536]{1,0:T(8,128)(2,1)S(1)}, u32[]{:S(2)}, u32[]{:S(2)}) collective-permute-start(bf16[128,1536]{1,0:T(8,128)(2,1)} %bitcast.39), channel_id=1, source_target_pairs={{0,1},{1,0},{2,3},{3,2},{4,5},{5,4},{6,7},{7,6},{8,9},{9,8},{10,11... | collective-permute-start | bytes 1179656 | tf_op jit(solution)/shard_map/ppermute | solution.py:271
  0.5 0.0 copy-start.5
  0.5 0.0 copy-start.6
  1.2 0.0 copy-start.3
  1.2 0.0 copy-start.4
  1.2 0.0 copy-done.5
  1.2 0.0 copy-done.6
  1.2 0.6 %copy-done.3 = s32[1,128,9]{1,0,2:T(1,128)S(1)} copy-done((s32[1,128,9]{1,0,2:T(1,128)S(1)}, s32[1,128,9]{1,0,2:T(1,128)}, u32[]{:S(2)}) %copy-start.3) | copy-done | bytes 4632
  1.9 0.0 copy-done.4
  1.9 0.1 concatenate.6.small_ref
  2.0 0.0 copy-start
  2.0 0.4 %shard_map.83 = (s32[9,128,128]{2,1,0:T(8,128)S(1)}, f32[4,128,128]{2,1,0:T(8,128)S(1)}, bf16[512,256]{1,0:T(8,128)(2,1)S(1)}) custom-call(f32[21,128]{1,0:T(8,128)S(1)} %concatenate.6.small_ref), custom_call_target="tpu_custom_call" | custom-call | flops 2000000000 | tf_op jit(solution)/shard_map/pallas_call | solution.py:253
  2.5 0.5 %copy-done = bf16[1,128,1536]{2,1,0:T(8,128)(2,1)S(1)} copy-done((bf16[1,128,1536]{2,1,0:T(8,128)(2,1)S(1)}, bf16[1,128,1536]{2,1,0:T(8,128)(2,1)}, u32[]{:S(2)}) %copy-start) | copy-done | bytes 393240
  3.0 0.0 copy-start.1
  3.0 0.0 copy-start.2
  3.0 0.4 %shard_map.84.filt_ref = f32[12,128,128]{2,1,0:T(8,128)S(1)} custom-call(bf16[128,1536]{1,0:T(8,128)(2,1)S(1)} %bitcast.40, bf16[512,256]{1,0:T(8,128)(2,1)S(1)} %get-tuple-element.12.band_ref), custom_call_target="tpu_custom_call" | custom-call | tf_op jit(solution)/shard_map/pallas_call | solution.py:253
  3.4 0.4 %copy-done.1 = s32[8,1,16,9]{2,1,3,0:T(1,128)S(1)} copy-done((s32[8,1,16,9]{2,1,3,0:T(1,128)S(1)}, s32[8,1,16,9]{2,1,3,0:T(1,128)}, u32[]{:S(2)}) %copy-start.1) | copy-done | bytes 4632
  3.8 0.0 copy-done.2
  3.8 0.0 collective-permute-done.other_ref
  3.8 1.5 %shard_map.86 = bf16[4,16,1536]{2,1,0:T(8,128)(2,1)S(1)} custom-call(bf16[128,1536]{1,0:T(8,128)(2,1)S(1)} %collective-permute-done.other_ref, s32[9,128,128]{2,1,0:T(8,128)S(1)} %get-tuple-element.13.place_ref, f32[4,128,128]{2,1,0:T(8,128)S(1)} %get-tuple-element.14.weight_ref, f32[12,128,128]{2,1,0:T(8,128)S(1)} %shard_map.84.filt_ref, ...), custom_call_target="tpu_custom_call" | custom-call | tf_op jit(solution)/shard_map/pallas_call | solution.py:253
  5.3 2.6 %collective-permute-start.7 = (bf16[16,1536]{1,0:T(8,128)(2,1)S(1)}, bf16[16,1536]{1,0:T(8,128)(2,1)S(1)}, u32[]{:S(2)}, u32[]{:S(2)}) collective-permute-start(bf16[16,1536]{1,0:T(8,128)(2,1)S(1)} %get-tuple-element.15), channel_id=1, source_target_pairs={{0,2},{2,0},{4,6},{6,4},{8,10},{10,8},{12,14},{14,12},{1,3},{3,1},... | collective-permute-start | bytes 147464 | tf_op jit(solution)/shard_map/ppermute | solution.py:341
  7.9 1.5 %collective-permute-start.6 = (bf16[16,1536]{1,0:T(8,128)(2,1)S(1)}, bf16[16,1536]{1,0:T(8,128)(2,1)S(1)}, u32[]{:S(2)}, u32[]{:S(2)}) collective-permute-start(bf16[16,1536]{1,0:T(8,128)(2,1)S(1)} %get-tuple-element.17), channel_id=1, source_target_pairs={{0,6},{2,4},{4,2},{6,0},{8,14},{10,12},{12,10},{14,8},{1,7},{3,5},... | collective-permute-start | bytes 147464 | tf_op jit(solution)/shard_map/ppermute | solution.py:341
  9.4 1.5 %shard_map.85 = bf16[4,16,1536]{2,1,0:T(8,128)(2,1)S(1)} custom-call(bf16[128,1536]{1,0:T(8,128)(2,1)S(1)} %collective-permute-done.other_ref, s32[9,128,128]{2,1,0:T(8,128)S(1)} %get-tuple-element.13.place_ref, f32[4,128,128]{2,1,0:T(8,128)S(1)} %get-tuple-element.14.weight_ref, f32[12,128,128]{2,1,0:T(8,128)S(1)} %shard_map.84.filt_ref, ...), custom_call_target="tpu_custom_call" | custom-call | tf_op jit(solution)/shard_map/pallas_call | solution.py:253
  10.9 0.1 collective-permute-start.5
  11.1 3.9 %collective-permute-start.4 = (bf16[16,1536]{1,0:T(8,128)(2,1)S(1)}, bf16[16,1536]{1,0:T(8,128)(2,1)S(1)}, u32[]{:S(2)}, u32[]{:S(2)}) collective-permute-start(bf16[16,1536]{1,0:T(8,128)(2,1)S(1)} %get-tuple-element.19), channel_id=1, source_target_pairs={{0,10},{2,8},{4,14},{6,12},{8,2},{10,0},{12,6},{14,4},{1,11},{3,9}... | collective-permute-start | bytes 147464 | tf_op jit(solution)/shard_map/ppermute | solution.py:341
  15.0 0.3 %collective-permute-start.3 = (bf16[16,1536]{1,0:T(8,128)(2,1)S(1)}, bf16[16,1536]{1,0:T(8,128)(2,1)S(1)}, u32[]{:S(2)}, u32[]{:S(2)}) collective-permute-start(bf16[16,1536]{1,0:T(8,128)(2,1)S(1)} %get-tuple-element.20), channel_id=1, source_target_pairs={{0,8},{2,10},{4,12},{6,14},{8,0},{10,2},{12,4},{14,6},{1,9},{3,11}... | collective-permute-start | bytes 147464 | tf_op jit(solution)/shard_map/ppermute | solution.py:341
  15.3 0.0 collective-permute-done.7.refs_1_
  15.3 3.5 %collective-permute-start.2 = (bf16[16,1536]{1,0:T(8,128)(2,1)S(1)}, bf16[16,1536]{1,0:T(8,128)(2,1)S(1)}, u32[]{:S(2)}, u32[]{:S(2)}) collective-permute-start(bf16[16,1536]{1,0:T(8,128)(2,1)S(1)} %get-tuple-element.21), channel_id=1, source_target_pairs={{0,14},{2,12},{4,10},{6,8},{8,6},{10,4},{12,2},{14,0},{1,15},{3,13... | collective-permute-start | bytes 147464 | tf_op jit(solution)/shard_map/ppermute | solution.py:341
  18.9 0.0 collective-permute-done.6.refs_1_
  18.9 0.1 collective-permute-start.1
  19.0 0.4 %shard_map.82 = (s32[8,8,16,128]{3,2,1,0:T(8,128)S(1)}, bf16[8,4,64,32]{3,2,1,0:T(8,128)(2,1)S(1)}) custom-call(f32[21,128]{1,0:T(8,128)S(1)} %concatenate.6.small_ref, f32[8,18,16]{2,1,0:T(8,128)S(1)} %pad_maximum_fusion.table_ref), custom_call_target="tpu_custom_call" | custom-call | tf_op jit(solution)/shard_map/pallas_call | solution.py:253
  19.5 1.2 %shard_map.87.refs_2_ = f32[8,16,1536]{2,1,0:T(8,128)S(1)} custom-call(s32[8,8,16,128]{3,2,1,0:T(8,128)S(1)} %get-tuple-element.10.place_ref, bf16[8,4,64,32]{3,2,1,0:T(8,128)(2,1)S(1)} %get-tuple-element.11.weight_ref, bf16[512,256]{1,0:T(8,128)(2,1)S(1)} %get-tuple-element.12.band_ref, bf16[16,1536]{1,0:T(8,128)(2,1)S(1)} %get-tuple-element.16.refs_0_, ...), custom_call_target="tpu_custom_call" | custom-call | tf_op jit(solution)/shard_map/pallas_call | solution.py:253
  20.7 0.0 collective-permute-done.5.refs_0_
  20.7 1.2 %shard_map.88.refs_2_ = f32[8,16,1536]{2,1,0:T(8,128)S(1)} custom-call(s32[8,8,16,128]{3,2,1,0:T(8,128)S(1)} %get-tuple-element.10.place_ref, bf16[8,4,64,32]{3,2,1,0:T(8,128)(2,1)S(1)} %get-tuple-element.11.weight_ref, bf16[512,256]{1,0:T(8,128)(2,1)S(1)} %get-tuple-element.12.band_ref, bf16[16,1536]{1,0:T(8,128)(2,1)S(1)} %collective-permute-done.5.refs_0_, ...), custom_call_target="tpu_custom_call" | custom-call | tf_op jit(solution)/shard_map/pallas_call | solution.py:253
  21.9 0.0 collective-permute-done.4.refs_1_
  21.9 0.2 collective-permute-done.3.refs_0_
  22.1 1.2 %shard_map.89.refs_2_ = f32[8,16,1536]{2,1,0:T(8,128)S(1)} custom-call(s32[8,8,16,128]{3,2,1,0:T(8,128)S(1)} %get-tuple-element.10.place_ref, bf16[8,4,64,32]{3,2,1,0:T(8,128)(2,1)S(1)} %get-tuple-element.11.weight_ref, bf16[512,256]{1,0:T(8,128)(2,1)S(1)} %get-tuple-element.12.band_ref, bf16[16,1536]{1,0:T(8,128)(2,1)S(1)} %collective-permute-done.3.refs_0_, ...), custom_call_target="tpu_custom_call" | custom-call | tf_op jit(solution)/shard_map/pallas_call | solution.py:253
  23.2 0.0 collective-permute-done.2.refs_1_
  23.2 1.5 %collective-permute-done.1.refs_0_ = bf16[16,1536]{1,0:T(8,128)(2,1)S(1)} collective-permute-done((bf16[16,1536]{1,0:T(8,128)(2,1)S(1)}, bf16[16,1536]{1,0:T(8,128)(2,1)S(1)}, u32[]{:S(2)}, u32[]{:S(2)}) %collective-permute-start.1) | collective-permute-done | bytes 49184 | tf_op jit(solution)/shard_map/ppermute | solution.py:341
  24.8 1.9 %shard_map.90 = bf16[8,16,1536]{2,1,0:T(8,128)(2,1)} custom-call(s32[8,8,16,128]{3,2,1,0:T(8,128)S(1)} %get-tuple-element.10.place_ref, bf16[8,4,64,32]{3,2,1,0:T(8,128)(2,1)S(1)} %get-tuple-element.11.weight_ref, bf16[512,256]{1,0:T(8,128)(2,1)S(1)} %get-tuple-element.12.band_ref, bf16[16,1536]{1,0:T(8,128)(2,1)S(1)} %collective-permute-done.1.refs_0_, ...), custom_call_target="tpu_custom_call" | custom-call | tf_op jit(solution)/shard_map/pallas_call | solution.py:253
  (8 shorter events, 0.1 us)
Async XLA Ops:
  0.0 3.8 %collective-permute-start = (bf16[128,1536]{1,0:T(8,128)(2,1)}, bf16[128,1536]{1,0:T(8,128)(2,1)S(1)}, u32[]{:S(2)}, u32[]{:S(2)}) collective-permute-start(bf16[128,1536]{1,0:T(8,128)(2,1)} %bitcast.39), channel_id=1, source_target_pairs={{0,1},{1,0},{2,3},{3,2},{4,5},{5,4},{6,7},{7,6},{8,9},{9,8},{10,11... | collective-permute-start | bytes 1179656 | tf_op jit(solution)/shard_map/ppermute | solution.py:271
  0.5 0.7 %copy-start.5 = (f32[9]{0:T(128)S(1)}, f32[9]{0:T(128)}, u32[]{:S(2)}) copy-start(f32[9]{0:T(128)} %param.14) | copy-start | bytes 112
  0.5 0.7 %copy-start.6 = (f32[9]{0:T(128)S(1)}, f32[9]{0:T(128)}, u32[]{:S(2)}) copy-start(f32[9]{0:T(128)} %param.15) | copy-start | bytes 112
  1.2 0.7 %copy-start.3 = (s32[1,128,9]{1,0,2:T(1,128)S(1)}, s32[1,128,9]{1,0,2:T(1,128)}, u32[]{:S(2)}) copy-start(s32[1,128,9]{1,0,2:T(1,128)} %param.10) | copy-start | bytes 13828
  1.2 0.7 %copy-start.4 = (s32[1,128,9]{1,0,2:T(1,128)S(1)}, s32[1,128,9]{1,0,2:T(1,128)}, u32[]{:S(2)}) copy-start(s32[1,128,9]{1,0,2:T(1,128)} %param.9) | copy-start | bytes 13828
  2.0 1.0 %copy-start = (bf16[1,128,1536]{2,1,0:T(8,128)(2,1)S(1)}, bf16[1,128,1536]{2,1,0:T(8,128)(2,1)}, u32[]{:S(2)}) copy-start(bf16[1,128,1536]{2,1,0:T(8,128)(2,1)} %param.8) | copy-start | bytes 1179652
  3.0 0.8 %copy-start.1 = (s32[8,1,16,9]{2,1,3,0:T(1,128)S(1)}, s32[8,1,16,9]{2,1,3,0:T(1,128)}, u32[]{:S(2)}) copy-start(s32[8,1,16,9]{2,1,3,0:T(1,128)} %param.13) | copy-start | bytes 13828
  3.0 0.8 %copy-start.2 = (s32[8,1,16,9]{2,1,3,0:T(1,128)S(1)}, s32[8,1,16,9]{2,1,3,0:T(1,128)}, u32[]{:S(2)}) copy-start(s32[8,1,16,9]{2,1,3,0:T(1,128)} %param.12) | copy-start | bytes 13828
  5.3 10.0 %collective-permute-start.7 = (bf16[16,1536]{1,0:T(8,128)(2,1)S(1)}, bf16[16,1536]{1,0:T(8,128)(2,1)S(1)}, u32[]{:S(2)}, u32[]{:S(2)}) collective-permute-start(bf16[16,1536]{1,0:T(8,128)(2,1)S(1)} %get-tuple-element.15), channel_id=1, source_target_pairs={{0,2},{2,0},{4,6},{6,4},{8,10},{10,8},{12,14},{14,12},{1,3},{3,1},... | collective-permute-start | bytes 147464 | tf_op jit(solution)/shard_map/ppermute | solution.py:341
  7.9 11.0 %collective-permute-start.6 = (bf16[16,1536]{1,0:T(8,128)(2,1)S(1)}, bf16[16,1536]{1,0:T(8,128)(2,1)S(1)}, u32[]{:S(2)}, u32[]{:S(2)}) collective-permute-start(bf16[16,1536]{1,0:T(8,128)(2,1)S(1)} %get-tuple-element.17), channel_id=1, source_target_pairs={{0,6},{2,4},{4,2},{6,0},{8,14},{10,12},{12,10},{14,8},{1,7},{3,5},... | collective-permute-start | bytes 147464 | tf_op jit(solution)/shard_map/ppermute | solution.py:341
  10.9 9.7 %collective-permute-start.5 = (bf16[16,1536]{1,0:T(8,128)(2,1)S(1)}, bf16[16,1536]{1,0:T(8,128)(2,1)S(1)}, u32[]{:S(2)}, u32[]{:S(2)}) collective-permute-start(bf16[16,1536]{1,0:T(8,128)(2,1)S(1)} %get-tuple-element.18), channel_id=1, source_target_pairs={{0,4},{2,6},{4,0},{6,2},{8,12},{10,14},{12,8},{14,10},{1,5},{3,7},... | collective-permute-start | bytes 147464 | tf_op jit(solution)/shard_map/ppermute | solution.py:341
  11.1 10.8 %collective-permute-start.4 = (bf16[16,1536]{1,0:T(8,128)(2,1)S(1)}, bf16[16,1536]{1,0:T(8,128)(2,1)S(1)}, u32[]{:S(2)}, u32[]{:S(2)}) collective-permute-start(bf16[16,1536]{1,0:T(8,128)(2,1)S(1)} %get-tuple-element.19), channel_id=1, source_target_pairs={{0,10},{2,8},{4,14},{6,12},{8,2},{10,0},{12,6},{14,4},{1,11},{3,9}... | collective-permute-start | bytes 147464 | tf_op jit(solution)/shard_map/ppermute | solution.py:341
  15.0 7.0 %collective-permute-start.3 = (bf16[16,1536]{1,0:T(8,128)(2,1)S(1)}, bf16[16,1536]{1,0:T(8,128)(2,1)S(1)}, u32[]{:S(2)}, u32[]{:S(2)}) collective-permute-start(bf16[16,1536]{1,0:T(8,128)(2,1)S(1)} %get-tuple-element.20), channel_id=1, source_target_pairs={{0,8},{2,10},{4,12},{6,14},{8,0},{10,2},{12,4},{14,6},{1,9},{3,11}... | collective-permute-start | bytes 147464 | tf_op jit(solution)/shard_map/ppermute | solution.py:341
  15.3 7.9 %collective-permute-start.2 = (bf16[16,1536]{1,0:T(8,128)(2,1)S(1)}, bf16[16,1536]{1,0:T(8,128)(2,1)S(1)}, u32[]{:S(2)}, u32[]{:S(2)}) collective-permute-start(bf16[16,1536]{1,0:T(8,128)(2,1)S(1)} %get-tuple-element.21), channel_id=1, source_target_pairs={{0,14},{2,12},{4,10},{6,8},{8,6},{10,4},{12,2},{14,0},{1,15},{3,13... | collective-permute-start | bytes 147464 | tf_op jit(solution)/shard_map/ppermute | solution.py:341
  18.9 5.9 %collective-permute-start.1 = (bf16[16,1536]{1,0:T(8,128)(2,1)S(1)}, bf16[16,1536]{1,0:T(8,128)(2,1)S(1)}, u32[]{:S(2)}, u32[]{:S(2)}) collective-permute-start(bf16[16,1536]{1,0:T(8,128)(2,1)S(1)} %get-tuple-element.22), channel_id=1, source_target_pairs={{0,12},{2,14},{4,8},{6,10},{8,4},{10,6},{12,0},{14,2},{1,13},{3,15... | collective-permute-start | bytes 147464 | tf_op jit(solution)/shard_map/ppermute | solution.py:341

commit v2 on v1

v2 whole, which is shorter than its diff:
```python
import functools
import math

import jax
import jax.numpy as jnp
from jax import lax
from jax.experimental import pallas as pl
from jax.experimental.pallas import tpu as pltpu
from jax.sharding import PartitionSpec as P


AR = 4
AS = 4
TRI = 2
KR = 9
KS = 9
LANES = 128
SUB = 8
EDGE = 16
F32 = jnp.float32
BF16 = jnp.bfloat16
I32 = jnp.int32
GRANT = 24 << 20


def iota(shape, axis):
    return lax.broadcasted_iota(I32, shape, axis)


def filter_band(width):
    height = width + 2 * LANES
    away = jnp.abs(iota((height, width), 1) - (iota((height, width), 0) - LANES))
    energy = float(sum((TRI - abs(m)) ** 2 for m in range(1 - TRI, TRI)))
    return (jnp.maximum(TRI - away, 0).astype(F32) / math.sqrt(energy)).astype(BF16)


def pair_of(blocks):
    return 2 if blocks % 2 == 0 else 1


def filtered(source, band, store):
    blocks = source.shape[1] // LANES
    step = pair_of(blocks)
    for b in range(0, blocks, step):
        low, high = max(b - 1, 0), min(b + step + 1, blocks)
        start = (low - b + 1) * LANES
        part = source[:, low * LANES : high * LANES]
        dot = jnp.dot(part, band[start : start + (high - low) * LANES, :], preferred_element_type=F32)
        value = dot.astype(BF16).astype(F32)
        for i in range(step):
            store(b + i, value[:, i * LANES : (i + 1) * LANES])


def filtered_few(source, band):
    rows, time = source.shape
    blank = jnp.zeros((rows, LANES), BF16)
    wide = jnp.concatenate([blank, source, blank], axis=1)
    stack = jnp.concatenate([wide[:, t : t + 3 * LANES] for t in range(0, time, LANES)], axis=0)
    dot = jnp.dot(stack, band[: 3 * LANES, :LANES], preferred_element_type=F32).astype(BF16).astype(F32)
    return [dot[i : i + rows] for i in range(0, dot.shape[0], rows)]


def spread(table, pick):
    dims = (((0,), (0,)), ((), ()))
    return lax.dot_general(table.astype(F32).astype(BF16), pick.astype(BF16), dims, preferred_element_type=F32)


def weight_parts(frac, taper, keep):
    two = jnp.where(keep, frac * (taper * (1.0 / 256.0)), 0.0)
    one = jnp.where(keep, taper, 0.0) - two
    parts = []
    for value in (one, two):
        high = value.astype(BF16).astype(F32)
        parts += [high, value - high]
    return parts


def shifted(load, place, blocks):
    index = place & (LANES - 1)
    here = place < LANES
    moved = [jnp.take_along_axis(load(b), index, axis=1, mode="promise_in_bounds") for b in range(blocks)]
    moved.append(jnp.zeros_like(moved[0]))
    return [jnp.where(here, moved[b], moved[b + 1]) for b in range(blocks)]


def sums(weights, taps, blocks, rows):
    first, second = [], []
    step = pair_of(blocks)
    for b in range(0, blocks, step):
        stack = jnp.concatenate(
            [jnp.concatenate([tap[b + i] for tap in taps], axis=0).astype(BF16) for i in range(step)], axis=1
        )
        dot = jnp.dot(weights, stack, preferred_element_type=F32)
        for i in range(step):
            cols = slice(i * LANES, (i + 1) * LANES)
            first.append(dot[:rows, cols] + dot[rows : 2 * rows, cols])
            second.append(dot[2 * rows : 3 * rows, cols] + dot[3 * rows :, cols])
    return first, second


def join(first, second):
    rolled = [pltpu.roll(v, LANES - 1, 1) for v in second] + [jnp.zeros_like(second[0])]
    inner = iota(second[0].shape, 1) < LANES - 1
    return [v + jnp.where(inner, rolled[b], rolled[b + 1]) for b, v in enumerate(first)]


def chosen(taper_ref, tap):
    value = jnp.zeros(tap.shape, F32)
    for a in range(taper_ref.shape[0]):
        value = jnp.where(tap == a, taper_ref[a], value)
    return value


def head_kernel(
    live_ref, taper_in, delay_in, frac_in, traces_in, place_ref, weight_ref, filt_ref, band_ref,
    taper_ref, delay_ref, frac_ref, traces_ref, sem,
):
    sources = (delay_in, frac_in, taper_in, traces_in)
    targets = (delay_ref, frac_ref, taper_ref, traces_ref)
    copies = [pltpu.make_async_copy(s, t, sem.at[i]) for i, (s, t) in enumerate(zip(sources, targets))]
    for copy in copies:
        copy.start()
    band_ref[...] = filter_band(band_ref.shape[1])
    for copy in copies[:3]:
        copy.wait()
    rows = delay_ref.shape[2]
    delay, frac = delay_ref[:, 0, :], frac_ref[:, 0, :]
    for a in range(KR):
        pick = iota((KR, LANES), 0) == a
        place_ref[a] = iota((rows, LANES), 1) + spread(delay, pick).astype(I32)
    wide = (rows, LANES)
    tap = iota((KR, LANES), 1) // SUB == iota((KR, LANES), 0)
    row, lane = iota(wide, 0), iota(wide, 1)
    line = row + lax.axis_index("rcv") * rows
    live = jnp.minimum(live_ref[0], rows * lax.axis_size("rcv"))
    source = line + lane // SUB - AR
    keep = (lane % SUB == row % SUB) & (lane < KR * SUB) & (source >= 0) & (source < live)
    fold = jnp.minimum(line + AR, live - 1) - jnp.maximum(line - AR, 0) + 1
    taper = chosen(taper_ref, iota((1, LANES), 1) // SUB)
    taper = taper / jnp.sqrt(jnp.maximum(fold, 1).astype(F32))
    for i, part in enumerate(weight_parts(spread(frac, tap), taper, keep)):
        weight_ref[i] = part

    def store(b, value):
        filt_ref[b] = value

    copies[3].wait()
    filtered(traces_ref[...], band_ref, store)


def receiver_kernel(far, peers, other_ref, place_ref, weight_ref, filt_ref, band_ref, out_ref, src_ref):
    blocks, rows = filt_ref.shape[:2]
    part = rows // 2
    per_peer = rows // peers
    me = lax.axis_index("shot")
    mine = me // (peers // 2)
    half = (1 - mine) if far else mine
    low = me % (peers // 2)
    base = pl.multiple_of(half * part, part)

    left_at = pl.ds(pl.multiple_of(jnp.maximum(base - EDGE, 0), EDGE), EDGE)
    right_at = pl.ds(pl.multiple_of(jnp.minimum(base + part, rows - EDGE), EDGE), EDGE)
    far_side = pl.multiple_of(jnp.where(half == 0, rows - EDGE, 0), EDGE)
    other = filtered_few(other_ref[pl.ds(far_side, EDGE), :], band_ref)
    for b in range(blocks):
        src_ref[b, :EDGE] = jnp.where(half == 0, other[b], filt_ref[b, left_at, :])
        src_ref[b, EDGE : EDGE + part] = filt_ref[b, pl.ds(base, part), :]
        src_ref[b, EDGE + part :] = jnp.where(half == 1, other[b], filt_ref[b, right_at, :])

    step = max(1, min(2, per_peer // SUB))
    count = part // (step * SUB)
    for c in range(count):
        totals = []
        for g in range(c * step, (c + 1) * step):
            at = pl.ds(pl.multiple_of(base + g * SUB, SUB), SUB)
            taps = []
            for a in range(KR):
                row = EDGE + g * SUB + a - AR
                taps.append(shifted(lambda b: src_ref[b, row : row + SUB, :], place_ref[a, at, :], blocks))
            weights = jnp.concatenate([weight_ref[i, at, : KR * SUB] for i in range(4)], axis=0).astype(BF16)
            totals.append(join(*sums(weights, taps, blocks, SUB)))
        first = c * step * SUB
        height = min(step * SUB, per_peer)
        for s in range(0, step * SUB, height):
            peer = ((first + s) // per_peer) ^ low
            start = (first + s) % per_peer
            for b in range(blocks):
                value = jnp.concatenate([t[b] for t in totals], axis=0).astype(BF16)
                out_ref[peer, start : start + height, b * LANES : (b + 1) * LANES] = value[s : s + height]


def source_tables_kernel(peers, share, calls, taper_in, delay_ref, frac_ref, place_ref, weight_ref, taper_ref, sem):
    rows = delay_ref.shape[2]
    me = lax.axis_index("shot")
    wide = share * rows
    copy = pltpu.make_async_copy(taper_in, taper_ref, sem)
    copy.start()
    copy.wait()

    def shot_of(groups, lane):
        shot = jnp.zeros_like(lane)
        for i, group in enumerate(groups):
            shot = jnp.where(lane // wide == i, ((me // share) ^ group) * share + (lane % wide) // rows, shot)
        return shot

    for k in range(peers):
        delay, frac = delay_ref[k], frac_ref[k]
        scale = 1.0 / math.sqrt(min(k + AS, peers - 1) - max(k - AS, 0) + 1)
        for p in range(peers):
            place = iota((rows, LANES), 1)
            if abs(p - k) <= AS:
                place = place + spread(delay, iota((KS, LANES), 0) == p - k + AS).astype(I32)
            place_ref[k, p] = place
        row, lane = iota((rows, LANES), 0), iota((rows, LANES), 1)
        for c, groups in enumerate(calls):
            used = len(groups) * wide
            tap = shot_of(groups, lane) - k + AS
            keep = (lane % rows == row) & (tap >= 0) & (tap < KS) & (lane < used)
            taper = chosen(taper_ref, shot_of(groups, iota((1, LANES), 1)) - k + AS)
            column = shot_of(groups, iota((KS, LANES), 1)) - k + AS
            parts = weight_parts(
                spread(frac, column == iota((KS, LANES), 0)), taper * scale, keep
            )
            weight_ref[c, k] = jnp.concatenate(parts, axis=0).astype(BF16)[:, :used]


def source_kernel(turn, last, peers, share, groups, place_ref, weight_ref, band_ref, *refs):
    used = len(groups) * share
    ins, refs = refs[:used], refs[used:]
    if turn:
        part_ref, refs = refs[0], refs[1:]
    if last:
        out_ref, src_ref, done_ref, sem = refs
    else:
        out_ref, src_ref = refs
    per_peer, time = ins[0].shape
    blocks = time // LANES
    me = lax.axis_index("shot")
    shots = [((me // share) ^ group) * share + e for group in groups for e in range(share)]
    slots = [i * share + ((me % share) ^ e) for i in range(len(groups)) for e in range(share)]

    def store(b, value):
        for i in range(used):
            src_ref[slots[i], b] = value[i * per_peer : (i + 1) * per_peer]

    filtered(jnp.concatenate([ref[...] for ref in ins], axis=0), band_ref, store)
    rows = min(SUB, per_peer)
    copies = []
    for k in range(peers):
        taps = []
        for i in range(used):
            for r in range(0, per_peer, rows):
                at = slice(r, r + rows)
                taps.append(shifted(lambda b: src_ref[i, b, at, :], place_ref[k, shots[i], at, :], blocks))
        pair = sums(weight_ref[turn, k], taps, blocks, per_peer)
        if turn:
            pair = [
                [v + part_ref[i, k, :, b * LANES : (b + 1) * LANES] for b, v in enumerate(part)]
                for i, part in enumerate(pair)
            ]
        if last:
            for b, value in enumerate(join(*pair)):
                done_ref[k, :, b * LANES : (b + 1) * LANES] = value.astype(BF16)
            copies.append(pltpu.make_async_copy(done_ref.at[k], out_ref.at[k], sem.at[k]))
            copies[-1].start()
        else:
            for i, part in enumerate(pair):
                for b, value in enumerate(part):
                    out_ref[i, k, :, b * LANES : (b + 1) * LANES] = value
    for copy in copies:
        copy.wait()


VMEM = pl.BlockSpec(memory_space=pltpu.VMEM)
SMEM = pl.BlockSpec(memory_space=pltpu.SMEM)
ANY = pl.BlockSpec(memory_space=pl.ANY)


def stay(value):
    return pltpu.with_memory_space_constraint(value, pltpu.HBM)


def call(kernel, args, outs, scratch=(), in_specs=None, out_specs=None):
    return pl.pallas_call(
        kernel,
        out_shape=outs,
        in_specs=in_specs or [VMEM] * len(args),
        out_specs=out_specs or ([VMEM] * len(outs) if isinstance(outs, tuple) else VMEM),
        scratch_shapes=list(scratch),
        compiler_params=pltpu.CompilerParams(vmem_limit_bytes=GRANT),
    )(*args)


def body(traces, rcv_delay, rcv_frac, live_count, src_delay, src_frac, rcv_taper, src_taper):
    rows, time = traces.shape[1:]
    blocks = time // LANES
    peers = lax.axis_size("shot")
    half_peers = peers // 2
    per_peer = rows // peers
    traces = traces[0]
    other = lax.ppermute(traces, "rcv", [(0, 1), (1, 0)])
    shape = jax.ShapeDtypeStruct
    width = pair_of(blocks) * LANES

    share = max(1, peers // 4)
    groups = list(range(peers // share))
    calls = [g for g in (groups[0::2], groups[1::2]) if g]
    delay, frac = (jnp.transpose(v, (2, 0, 1)) for v in (rcv_delay, rcv_frac))
    place, weight, filt, band = call(
        head_kernel,
        [live_count, *(stay(v) for v in (rcv_taper, delay, frac, traces))],
        (
            shape((KR, rows, LANES), I32),
            shape((4, rows, LANES), F32),
            shape((blocks, rows, LANES), F32),
            shape((width + 2 * LANES, width), BF16),
        ),
        [
            pltpu.SMEM(rcv_taper.shape, F32),
            pltpu.VMEM(delay.shape, I32),
            pltpu.VMEM(frac.shape, I32),
            pltpu.VMEM(traces.shape, BF16),
            pltpu.SemaphoreType.DMA((4,)),
        ],
        in_specs=[SMEM] + [ANY] * 4,
    )

    def receivers(far):
        return call(
            functools.partial(receiver_kernel, far, peers),
            (other, place, weight, filt, band),
            shape((half_peers, per_peer, time), BF16),
            [pltpu.VMEM((blocks, rows // 2 + 2 * EDGE, LANES), F32)],
        )

    far_out = receivers(1)
    far_in = [swap(far_out[r], r + half_peers, peers) for r in range(half_peers)]
    near_out = receivers(0)
    near_in = [near_out[0]] + [swap(near_out[r], r, peers) for r in range(1, half_peers)]

    tables = [jnp.transpose(v[:, 0], (0, 2, 1)) for v in (src_delay, src_frac)]
    source_tables = call(
        functools.partial(source_tables_kernel, peers, share, calls),
        (stay(src_taper), *tables),
        (
            shape((peers, peers, per_peer, LANES), I32),
            shape((len(calls), peers, 4 * per_peer, len(calls[0]) * share * per_peer), BF16),
        ),
        [pltpu.SMEM(src_taper.shape, F32), pltpu.SemaphoreType.DMA],
        in_specs=[ANY, VMEM, VMEM],
    )
    arrived = near_in + far_in
    result = None
    for turn, groups in enumerate(calls):
        last = turn == len(calls) - 1
        extra = [] if turn == 0 else [result]
        ins = [arrived[g * share + e] for g in groups for e in range(share)]
        scratch = [pltpu.VMEM((len(ins), blocks, per_peer, LANES), F32)]
        if last:
            scratch += [pltpu.VMEM((peers, per_peer, time), BF16), pltpu.SemaphoreType.DMA((peers,))]
        result = call(
            functools.partial(source_kernel, turn, last, peers, share, groups),
            (*source_tables, band, *ins, *extra),
            shape((peers, per_peer, time), BF16) if last else shape((2, peers, per_peer, time), F32),
            scratch,
            out_specs=ANY if last else VMEM,
        )
    return result.reshape(peers, 1, per_peer, time)


def swap(block, step, peers):
    return lax.ppermute(block, "shot", [(i, i ^ step) for i in range(peers)])


def solution(mesh):
    return jax.shard_map(
        body,
        mesh=mesh,
        in_specs=(
            P(("slab", "shot"), "rcv", None),
            P(("slab", "shot"), "rcv", None),
            P(("slab", "shot"), "rcv", None),
            P(("slab", "shot")),
            P("slab", "rcv", "shot", None),
            P("slab", "rcv", "shot", None),
            P(),
            P(),
        ),
        out_specs=P("slab", "rcv", "shot", None),
        check_vma=False,
    )
```

time: 26.9 us -> 23.9 us (0.89)
  local copies, waits for them, and re-layouts: 1.77 us -> 0.05 us
  Pallas kernels: 9.59 us -> 8.84 us
  waiting for transfers between devices: 1.76 us -> 1.48 us
    unnamed x14 -> x4, local copies, waits for them, and re-layouts: 1.59 us -> 0.01 us
    pallas_call x9 -> x6, Pallas kernels: 9.59 us -> 8.84 us  [call(): pl.pallas_call(kernel, out_shape=outs, in_specs=in_specs or [VMEM] * len(...]
    ppermute x7, waiting for transfers between devices: 1.76 us -> 1.48 us  [swap(): return lax.ppermute(block, 'shot', [(i, i ^ step) for i in range(peers)])]
  transfers between devices with their start and end apart: 8 -> 8, of which waited for: 2 -> 1; matrix products, arithmetic and copies ran while one was open for 1% -> 0% of each run, Pallas kernels for 23% -> 22%
where the time goes in v2:
time: 23.9 us; the launch traced here: 23.7 us
  starting transfers between devices  12.6 us (53%)
  Pallas kernels  8.84 us (37%)
  waiting for transfers between devices  1.48 us (6%)
  between operations  0.73 us (3%)
    ppermute x7, starting transfers between devices, swap(): return lax.ppermute(block, 'shot', [(i, i ^ step) for i in range(peers)])  12.1 us
    pallas_call x6, Pallas kernels, call(): pl.pallas_call(kernel, out_shape=outs, in_specs=in_specs or [VMEM] * len(...  8.84 us
    ppermute x7, waiting for transfers between devices, swap(): return lax.ppermute(block, 'shot', [(i, i ^ step) for i in range(peers)])  1.48 us
    ppermute x1, starting transfers between devices, body(): other = lax.ppermute(traces, 'rcv', [(0, 1), (1, 0)])  0.49 us
  transfers between devices with their start and end apart: 8, of which 1 were waited for; matrix products, arithmetic and copies ran while one was open for 0% of the time, Pallas kernels for 22%

profile of v2, /device:TPU:0, one launch (start us, length us, event | category | flops | bytes accessed | tf_op | source)
XLA Modules:
  0.0 23.7 jit_solution(8062820275436680486)
XLA Ops:
  0.0 0.5 %collective-permute-start = (bf16[128,1536]{1,0:T(8,128)(2,1)}, bf16[128,1536]{1,0:T(8,128)(2,1)S(1)}, u32[]{:S(2)}, u32[]{:S(2)}) collective-permute-start(bf16[128,1536]{1,0:T(8,128)(2,1)} %bitcast.32), channel_id=1, source_target_pairs={{0,1},{1,0},{2,3},{3,2},{4,5},{5,4},{6,7},{7,6},{8,9},{9,8},{10,11... | collective-permute-start | bytes 1179656 | tf_op jit(solution)/shard_map/ppermute | solution.py:301
  1.1 1.5 %shard_map.83 = (s32[9,128,128]{2,1,0:T(8,128)S(1)}, f32[4,128,128]{2,1,0:T(8,128)S(1)}, f32[12,128,128]{2,1,0:T(8,128)S(1)}, bf16[512,256]{1,0:T(8,128)(2,1)S(1)}) custom-call(s32[1]{0:T(128)S(6)} %copy.19.live_ref, f32[9]{0:T(128)} %taper_in.3, s32[9,1,128]{2,1,0:T(1,128)} %bitcast.34, s32[9,1,128]{2,1,0:T(1,128)} %bitcast.35, bf16[128,1536]{1,0:T(8,128)(2,1)} %bitcast.33), custom_call_target="tpu_custom_call" | custom-call | tf_op jit(solution)/shard_map/pallas_call | solution.py:284
  2.7 0.0 collective-permute-done.other_ref
  2.7 1.5 %shard_map.85 = bf16[4,16,1536]{2,1,0:T(8,128)(2,1)S(1)} custom-call(bf16[128,1536]{1,0:T(8,128)(2,1)S(1)} %collective-permute-done.other_ref, s32[9,128,128]{2,1,0:T(8,128)S(1)} %get-tuple-element.14.place_ref, f32[4,128,128]{2,1,0:T(8,128)S(1)} %get-tuple-element.15.weight_ref, f32[12,128,128]{2,1,0:T(8,128)S(1)} %get-tuple-element.16.filt_ref, ...), custom_call_target="tpu_custom_call" | custom-call | tf_op jit(solution)/shard_map/pallas_call | solution.py:284
  4.2 0.0 copy-start
  4.2 0.0 copy-start.1
  4.2 3.6 %collective-permute-start.6 = (bf16[16,1536]{1,0:T(8,128)(2,1)S(1)}, bf16[16,1536]{1,0:T(8,128)(2,1)S(1)}, u32[]{:S(2)}, u32[]{:S(2)}) collective-permute-start(bf16[16,1536]{1,0:T(8,128)(2,1)S(1)} %get-tuple-element.18), channel_id=1, source_target_pairs={{0,8},{2,10},{4,12},{6,14},{8,0},{10,2},{12,4},{14,6},{1,9},{3,11}... | collective-permute-start | bytes 147464 | tf_op jit(solution)/shard_map/ppermute | solution.py:372
  7.9 1.3 %collective-permute-start.7 = (bf16[16,1536]{1,0:T(8,128)(2,1)S(1)}, bf16[16,1536]{1,0:T(8,128)(2,1)S(1)}, u32[]{:S(2)}, u32[]{:S(2)}) collective-permute-start(bf16[16,1536]{1,0:T(8,128)(2,1)S(1)} %get-tuple-element.17), channel_id=1, source_target_pairs={{0,10},{2,8},{4,14},{6,12},{8,2},{10,0},{12,6},{14,4},{1,11},{3,9}... | collective-permute-start | bytes 147464 | tf_op jit(solution)/shard_map/ppermute | solution.py:372
  9.2 1.5 %shard_map.84 = bf16[4,16,1536]{2,1,0:T(8,128)(2,1)S(1)} custom-call(bf16[128,1536]{1,0:T(8,128)(2,1)S(1)} %collective-permute-done.other_ref, s32[9,128,128]{2,1,0:T(8,128)S(1)} %get-tuple-element.14.place_ref, f32[4,128,128]{2,1,0:T(8,128)S(1)} %get-tuple-element.15.weight_ref, f32[12,128,128]{2,1,0:T(8,128)S(1)} %get-tuple-element.16.filt_ref, ...), custom_call_target="tpu_custom_call" | custom-call | tf_op jit(solution)/shard_map/pallas_call | solution.py:284
  10.7 0.3 %collective-permute-start.5 = (bf16[16,1536]{1,0:T(8,128)(2,1)S(1)}, bf16[16,1536]{1,0:T(8,128)(2,1)S(1)}, u32[]{:S(2)}, u32[]{:S(2)}) collective-permute-start(bf16[16,1536]{1,0:T(8,128)(2,1)S(1)} %get-tuple-element.21), channel_id=1, source_target_pairs={{0,2},{2,0},{4,6},{6,4},{8,10},{10,8},{12,14},{14,12},{1,3},{3,1},... | collective-permute-start | bytes 147464 | tf_op jit(solution)/shard_map/ppermute | solution.py:372
  11.0 3.9 %collective-permute-start.3 = (bf16[16,1536]{1,0:T(8,128)(2,1)S(1)}, bf16[16,1536]{1,0:T(8,128)(2,1)S(1)}, u32[]{:S(2)}, u32[]{:S(2)}) collective-permute-start(bf16[16,1536]{1,0:T(8,128)(2,1)S(1)} %get-tuple-element.20), channel_id=1, source_target_pairs={{0,12},{2,14},{4,8},{6,10},{8,4},{10,6},{12,0},{14,2},{1,13},{3,15... | collective-permute-start | bytes 147464 | tf_op jit(solution)/shard_map/ppermute | solution.py:372
  14.8 1.2 %collective-permute-start.4 = (bf16[16,1536]{1,0:T(8,128)(2,1)S(1)}, bf16[16,1536]{1,0:T(8,128)(2,1)S(1)}, u32[]{:S(2)}, u32[]{:S(2)}) collective-permute-start(bf16[16,1536]{1,0:T(8,128)(2,1)S(1)} %get-tuple-element.19), channel_id=1, source_target_pairs={{0,14},{2,12},{4,10},{6,8},{8,6},{10,4},{12,2},{14,0},{1,15},{3,13... | collective-permute-start | bytes 147464 | tf_op jit(solution)/shard_map/ppermute | solution.py:372
  16.0 0.0 collective-permute-done.6.refs_2_
  16.0 0.0 collective-permute-start.1
  16.0 0.0 collective-permute-done.7.refs_3_
  16.0 1.8 %collective-permute-start.2 = (bf16[16,1536]{1,0:T(8,128)(2,1)S(1)}, bf16[16,1536]{1,0:T(8,128)(2,1)S(1)}, u32[]{:S(2)}, u32[]{:S(2)}) collective-permute-start(bf16[16,1536]{1,0:T(8,128)(2,1)S(1)} %get-tuple-element.23), channel_id=1, source_target_pairs={{0,6},{2,4},{4,2},{6,0},{8,14},{10,12},{12,10},{14,8},{1,7},{3,5},... | collective-permute-start | bytes 147464 | tf_op jit(solution)/shard_map/ppermute | solution.py:372
  17.8 0.0 copy-done
  17.8 0.0 copy-done.1
  17.8 1.0 %shard_map.82 = (s32[8,8,16,128]{3,2,1,0:T(8,128)S(1)}, bf16[2,8,64,64]{3,2,1,0:T(8,128)(2,1)S(1)}) custom-call(f32[9]{0:T(128)} %taper_in.2, s32[8,9,16]{2,1,0:T(8,128)S(1)} %get-tuple-element.26.delay_ref, s32[8,9,16]{2,1,0:T(8,128)S(1)} %get-tuple-element.25.frac_ref), custom_call_target="tpu_custom_call" | custom-call | tf_op jit(solution)/shard_map/pallas_call | solution.py:284
  18.9 0.0 collective-permute-done.5.refs_1_
  18.9 1.3 %shard_map.86.refs_4_ = f32[2,8,16,1536]{3,2,1,0:T(8,128)S(1)} custom-call(s32[8,8,16,128]{3,2,1,0:T(8,128)S(1)} %get-tuple-element.11.place_ref, bf16[2,8,64,64]{3,2,1,0:T(8,128)(2,1)S(1)} %get-tuple-element.12.weight_ref, bf16[512,256]{1,0:T(8,128)(2,1)S(1)} %get-tuple-element.13.band_ref, bf16[16,1536]{1,0:T(8,128)(2,1)S(1)} %get-tuple-element.22.refs_0_, ...), custom_call_target="tpu_custom_call" | custom-call | tf_op jit(solution)/shard_map/pallas_call | solution.py:284
  20.1 0.0 collective-permute-done.3.refs_2_
  20.2 1.5 %collective-permute-done.4.refs_3_ = bf16[16,1536]{1,0:T(8,128)(2,1)S(1)} collective-permute-done((bf16[16,1536]{1,0:T(8,128)(2,1)S(1)}, bf16[16,1536]{1,0:T(8,128)(2,1)S(1)}, u32[]{:S(2)}, u32[]{:S(2)}) %collective-permute-start.4) | collective-permute-done | bytes 49184 | tf_op jit(solution)/shard_map/ppermute | solution.py:372
  21.6 0.0 collective-permute-done.1.refs_0_
  21.6 0.0 collective-permute-done.2.refs_1_
  21.6 2.1 %shard_map.87 = bf16[8,16,1536]{2,1,0:T(8,128)(2,1)} custom-call(s32[8,8,16,128]{3,2,1,0:T(8,128)S(1)} %get-tuple-element.11.place_ref, bf16[2,8,64,64]{3,2,1,0:T(8,128)(2,1)S(1)} %get-tuple-element.12.weight_ref, bf16[512,256]{1,0:T(8,128)(2,1)S(1)} %get-tuple-element.13.band_ref, bf16[16,1536]{1,0:T(8,128)(2,1)S(1)} %collective-permute-done.1.refs_0_, ...), custom_call_target="tpu_custom_call" | custom-call | tf_op jit(solution)/shard_map/pallas_call | solution.py:284
  (3 shorter events, 0.0 us)
Async XLA Ops:
  0.0 2.7 %collective-permute-start = (bf16[128,1536]{1,0:T(8,128)(2,1)}, bf16[128,1536]{1,0:T(8,128)(2,1)S(1)}, u32[]{:S(2)}, u32[]{:S(2)}) collective-permute-start(bf16[128,1536]{1,0:T(8,128)(2,1)} %bitcast.32), channel_id=1, source_target_pairs={{0,1},{1,0},{2,3},{3,2},{4,5},{5,4},{6,7},{7,6},{8,9},{9,8},{10,11... | collective-permute-start | bytes 1179656 | tf_op jit(solution)/shard_map/ppermute | solution.py:301
  4.2 13.6 %copy-start = (s32[8,1,16,9]{2,1,3,0:T(1,128)S(1)}, s32[8,1,16,9]{2,1,3,0:T(1,128)}, u32[]{:S(2)}) copy-start(s32[8,1,16,9]{2,1,3,0:T(1,128)} %param.13) | copy-start | bytes 13828
  4.2 13.6 %copy-start.1 = (s32[8,1,16,9]{2,1,3,0:T(1,128)S(1)}, s32[8,1,16,9]{2,1,3,0:T(1,128)}, u32[]{:S(2)}) copy-start(s32[8,1,16,9]{2,1,3,0:T(1,128)} %param.12) | copy-start | bytes 13828
  4.2 11.8 %collective-permute-start.6 = (bf16[16,1536]{1,0:T(8,128)(2,1)S(1)}, bf16[16,1536]{1,0:T(8,128)(2,1)S(1)}, u32[]{:S(2)}, u32[]{:S(2)}) collective-permute-start(bf16[16,1536]{1,0:T(8,128)(2,1)S(1)} %get-tuple-element.18), channel_id=1, source_target_pairs={{0,8},{2,10},{4,12},{6,14},{8,0},{10,2},{12,4},{14,6},{1,9},{3,11}... | collective-permute-start | bytes 147464 | tf_op jit(solution)/shard_map/ppermute | solution.py:372
  7.9 8.2 %collective-permute-start.7 = (bf16[16,1536]{1,0:T(8,128)(2,1)S(1)}, bf16[16,1536]{1,0:T(8,128)(2,1)S(1)}, u32[]{:S(2)}, u32[]{:S(2)}) collective-permute-start(bf16[16,1536]{1,0:T(8,128)(2,1)S(1)} %get-tuple-element.17), channel_id=1, source_target_pairs={{0,10},{2,8},{4,14},{6,12},{8,2},{10,0},{12,6},{14,4},{1,11},{3,9}... | collective-permute-start | bytes 147464 | tf_op jit(solution)/shard_map/ppermute | solution.py:372
  10.7 8.2 %collective-permute-start.5 = (bf16[16,1536]{1,0:T(8,128)(2,1)S(1)}, bf16[16,1536]{1,0:T(8,128)(2,1)S(1)}, u32[]{:S(2)}, u32[]{:S(2)}) collective-permute-start(bf16[16,1536]{1,0:T(8,128)(2,1)S(1)} %get-tuple-element.21), channel_id=1, source_target_pairs={{0,2},{2,0},{4,6},{6,4},{8,10},{10,8},{12,14},{14,12},{1,3},{3,1},... | collective-permute-start | bytes 147464 | tf_op jit(solution)/shard_map/ppermute | solution.py:372
  11.0 9.2 %collective-permute-start.3 = (bf16[16,1536]{1,0:T(8,128)(2,1)S(1)}, bf16[16,1536]{1,0:T(8,128)(2,1)S(1)}, u32[]{:S(2)}, u32[]{:S(2)}) collective-permute-start(bf16[16,1536]{1,0:T(8,128)(2,1)S(1)} %get-tuple-element.20), channel_id=1, source_target_pairs={{0,12},{2,14},{4,8},{6,10},{8,4},{10,6},{12,0},{14,2},{1,13},{3,15... | collective-permute-start | bytes 147464 | tf_op jit(solution)/shard_map/ppermute | solution.py:372
  14.8 6.8 %collective-permute-start.4 = (bf16[16,1536]{1,0:T(8,128)(2,1)S(1)}, bf16[16,1536]{1,0:T(8,128)(2,1)S(1)}, u32[]{:S(2)}, u32[]{:S(2)}) collective-permute-start(bf16[16,1536]{1,0:T(8,128)(2,1)S(1)} %get-tuple-element.19), channel_id=1, source_target_pairs={{0,14},{2,12},{4,10},{6,8},{8,6},{10,4},{12,2},{14,0},{1,15},{3,13... | collective-permute-start | bytes 147464 | tf_op jit(solution)/shard_map/ppermute | solution.py:372
  16.0 5.6 %collective-permute-start.1 = (bf16[16,1536]{1,0:T(8,128)(2,1)S(1)}, bf16[16,1536]{1,0:T(8,128)(2,1)S(1)}, u32[]{:S(2)}, u32[]{:S(2)}) collective-permute-start(bf16[16,1536]{1,0:T(8,128)(2,1)S(1)} %get-tuple-element.24), channel_id=1, source_target_pairs={{0,4},{2,6},{4,0},{6,2},{8,12},{10,14},{12,8},{14,10},{1,5},{3,7},... | collective-permute-start | bytes 147464 | tf_op jit(solution)/shard_map/ppermute | solution.py:372
  16.0 5.6 %collective-permute-start.2 = (bf16[16,1536]{1,0:T(8,128)(2,1)S(1)}, bf16[16,1536]{1,0:T(8,128)(2,1)S(1)}, u32[]{:S(2)}, u32[]{:S(2)}) collective-permute-start(bf16[16,1536]{1,0:T(8,128)(2,1)S(1)} %get-tuple-element.23), channel_id=1, source_target_pairs={{0,6},{2,4},{4,2},{6,0},{8,14},{10,12},{12,10},{14,8},{1,7},{3,5},... | collective-permute-start | bytes 147464 | tf_op jit(solution)/shard_map/ppermute | solution.py:372

commit v3 on v2

--- a/solution.py
+++ b/solution.py
@@ -17,6 +17,7 @@
 LANES = 128
 SUB = 8
 EDGE = 16
+PIECES = 4
 F32 = jnp.float32
 BF16 = jnp.bfloat16
 I32 = jnp.int32
@@ -28,10 +29,14 @@
 
 
 def filter_band(width):
-    height = width + 2 * LANES
-    away = jnp.abs(iota((height, width), 1) - (iota((height, width), 0) - LANES))
+    size = (3 * LANES, LANES)
+    away = jnp.abs(iota(size, 1) - (iota(size, 0) - LANES))
     energy = float(sum((TRI - abs(m)) ** 2 for m in range(1 - TRI, TRI)))
-    return (jnp.maximum(TRI - away, 0).astype(F32) / math.sqrt(energy)).astype(BF16)
+    one = (jnp.maximum(TRI - away, 0).astype(F32) / math.sqrt(energy)).astype(BF16)
+    blank = jnp.zeros((LANES, LANES), BF16)
+    count = width // LANES
+    columns = [jnp.concatenate([blank] * i + [one] + [blank] * (count - 1 - i), axis=0) for i in range(count)]
+    return jnp.concatenate(columns, axis=1)
 
 
 def pair_of(blocks):
@@ -39,16 +44,15 @@
 
 
 def filtered(source, band, store):
-    blocks = source.shape[1] // LANES
-    step = pair_of(blocks)
-    for b in range(0, blocks, step):
-        low, high = max(b - 1, 0), min(b + step + 1, blocks)
-        start = (low - b + 1) * LANES
-        part = source[:, low * LANES : high * LANES]
-        dot = jnp.dot(part, band[start : start + (high - low) * LANES, :], preferred_element_type=F32)
-        value = dot.astype(BF16).astype(F32)
-        for i in range(step):
-            store(b + i, value[:, i * LANES : (i + 1) * LANES])
+    rows, time = source.shape
+    high, wide = band.shape
+    blank = jnp.zeros((rows, LANES), BF16)
+    padded = jnp.concatenate([blank, source, blank], axis=1)
+    stack = jnp.concatenate([padded[:, t : t + high] for t in range(0, time, wide)], axis=0)
+    dot = jnp.dot(stack, band[...], preferred_element_type=F32).astype(BF16).astype(F32)
+    for i, t in enumerate(range(0, time, wide)):
+        for j in range(0, wide, LANES):
+            store((t + j) // LANES, dot[i * rows : (i + 1) * rows, j : j + LANES])
 
 
 def filtered_few(source, band):
@@ -112,18 +116,22 @@
 
 
 def head_kernel(
-    live_ref, taper_in, delay_in, frac_in, traces_in, place_ref, weight_ref, filt_ref, band_ref,
-    taper_ref, delay_ref, frac_ref, traces_ref, sem,
+    live_ref, taper_in, source_taper_in, delay_in, frac_in, traces_in,
+    place_ref, weight_ref, filt_ref, band_ref, source_taper_out, taper_ref, source_taper_ref, delay_ref, frac_ref, traces_ref, sem,
 ):
-    sources = (delay_in, frac_in, taper_in, traces_in)
-    targets = (delay_ref, frac_ref, taper_ref, traces_ref)
-    copies = [pltpu.make_async_copy(s, t, sem.at[i]) for i, (s, t) in enumerate(zip(sources, targets))]
+    pairs = [(delay_in, delay_ref), (frac_in, frac_ref), (taper_in, taper_ref), (source_taper_in, source_taper_ref)]
+    height = traces_in.shape[0] // PIECES
+    for i in range(PIECES):
+        at = pl.ds(i * height, height)
+        pairs.append((traces_in.at[at], traces_ref.at[at]))
+    copies = [pltpu.make_async_copy(s, t, sem.at[i]) for i, (s, t) in enumerate(pairs)]
     for copy in copies:
         copy.start()
     band_ref[...] = filter_band(band_ref.shape[1])
-    for copy in copies[:3]:
+    for copy in copies[:4]:
         copy.wait()
     rows = delay_ref.shape[2]
+    source_taper_out[...] = chosen(source_taper_ref, iota((SUB, LANES), 1))
     delay, frac = delay_ref[:, 0, :], frac_ref[:, 0, :]
     for a in range(KR):
         pick = iota((KR, LANES), 0) == a
@@ -135,16 +143,23 @@
     live = jnp.minimum(live_ref[0], rows * lax.axis_size("rcv"))
     source = line + lane // SUB - AR
     keep = (lane % SUB == row % SUB) & (lane < KR * SUB) & (source >= 0) & (source < live)
-    fold = jnp.minimum(line + AR, live - 1) - jnp.maximum(line - AR, 0) + 1
-    taper = chosen(taper_ref, iota((1, LANES), 1) // SUB)
-    taper = taper / jnp.sqrt(jnp.maximum(fold, 1).astype(F32))
+    place = iota((1, rows), 1) + lax.axis_index("rcv") * rows
+    fold = jnp.minimum(place + AR, live - 1) - jnp.maximum(place - AR, 0) + 1
+    rest = 1.0 / jnp.sqrt(jnp.maximum(fold, 1).astype(F32))
+    scale = jnp.zeros(wide, F32)
+    for _ in range(3):
+        part = rest.astype(BF16).astype(F32)
+        rest = rest - part
+        scale = scale + spread(part, iota((1, LANES), 1) >= 0)
+    taper = chosen(taper_ref, iota((1, LANES), 1) // SUB) * scale
     for i, part in enumerate(weight_parts(spread(frac, tap), taper, keep)):
         weight_ref[i] = part
 
     def store(b, value):
         filt_ref[b] = value
 
-    copies[3].wait()
+    for copy in copies[4:]:
+        copy.wait()
     filtered(traces_ref[...], band_ref, store)
 
 
@@ -189,13 +204,16 @@
                 out_ref[peer, start : start + height, b * LANES : (b + 1) * LANES] = value[s : s + height]
 
 
-def source_tables_kernel(peers, share, calls, taper_in, delay_ref, frac_ref, place_ref, weight_ref, taper_ref, sem):
+def source_tables_kernel(peers, share, calls, taper_ref, delay_ref, frac_ref, place_ref, weight_ref):
     rows = delay_ref.shape[2]
     me = lax.axis_index("shot")
     wide = share * rows
-    copy = pltpu.make_async_copy(taper_in, taper_ref, sem)
-    copy.start()
-    copy.wait()
+    for k in range(peers):
+        for p in range(peers):
+            place = iota((rows, LANES), 1)
+            if abs(p - k) <= AS:
+                place = place + spread(delay_ref[k], iota((KS, LANES), 0) == p - k + AS).astype(I32)
+            place_ref[k, p] = place
 
     def shot_of(groups, lane):
         shot = jnp.zeros_like(lane)
@@ -204,24 +222,20 @@
         return shot
 
     for k in range(peers):
-        delay, frac = delay_ref[k], frac_ref[k]
+        frac = frac_ref[k]
         scale = 1.0 / math.sqrt(min(k + AS, peers - 1) - max(k - AS, 0) + 1)
-        for p in range(peers):
-            place = iota((rows, LANES), 1)
-            if abs(p - k) <= AS:
-                place = place + spread(delay, iota((KS, LANES), 0) == p - k + AS).astype(I32)
-            place_ref[k, p] = place
         row, lane = iota((rows, LANES), 0), iota((rows, LANES), 1)
         for c, groups in enumerate(calls):
             used = len(groups) * wide
             tap = shot_of(groups, lane) - k + AS
             keep = (lane % rows == row) & (tap >= 0) & (tap < KS) & (lane < used)
-            taper = chosen(taper_ref, shot_of(groups, iota((1, LANES), 1)) - k + AS)
+            index = jnp.clip(shot_of(groups, iota((SUB, LANES), 1)) - k + AS, 0, KS - 1)
+            taper = jnp.take_along_axis(taper_ref[...], index, axis=1, mode="promise_in_bounds")[:1]
             column = shot_of(groups, iota((KS, LANES), 1)) - k + AS
             parts = weight_parts(
                 spread(frac, column == iota((KS, LANES), 0)), taper * scale, keep
             )
-            weight_ref[c, k] = jnp.concatenate(parts, axis=0).astype(BF16)[:, :used]
+            weight_ref[c, k, :, :used] = jnp.concatenate(parts, axis=0).astype(BF16)[:, :used]
 
 
 def source_kernel(turn, last, peers, share, groups, place_ref, weight_ref, band_ref, *refs):
@@ -252,7 +266,7 @@
             for r in range(0, per_peer, rows):
                 at = slice(r, r + rows)
                 taps.append(shifted(lambda b: src_ref[i, b, at, :], place_ref[k, shots[i], at, :], blocks))
-        pair = sums(weight_ref[turn, k], taps, blocks, per_peer)
+        pair = sums(weight_ref[turn, k, :, : used * per_peer], taps, blocks, per_peer)
         if turn:
             pair = [
                 [v + part_ref[i, k, :, b * LANES : (b + 1) * LANES] for b, v in enumerate(part)]
@@ -302,27 +316,32 @@
     shape = jax.ShapeDtypeStruct
     width = pair_of(blocks) * LANES
 
-    share = max(1, peers // 4)
+    share = 1
     groups = list(range(peers // share))
-    calls = [g for g in (groups[0::2], groups[1::2]) if g]
+    cut = half_peers // 2
+    early = groups[:cut] + groups[half_peers : half_peers + cut]
+    late = groups[half_peers - 1 : half_peers]
+    calls = [g for g in (early, [g for g in groups if g not in early + late], late) if g]
     delay, frac = (jnp.transpose(v, (2, 0, 1)) for v in (rcv_delay, rcv_frac))
-    place, weight, filt, band = call(
+    place, weight, filt, band, source_taper = call(
         head_kernel,
-        [live_count, *(stay(v) for v in (rcv_taper, delay, frac, traces))],
+        [live_count, *(stay(v) for v in (rcv_taper, src_taper, delay, frac, traces))],
         (
             shape((KR, rows, LANES), I32),
             shape((4, rows, LANES), F32),
             shape((blocks, rows, LANES), F32),
             shape((width + 2 * LANES, width), BF16),
+            shape((SUB, LANES), F32),
         ),
         [
             pltpu.SMEM(rcv_taper.shape, F32),
+            pltpu.SMEM(src_taper.shape, F32),
             pltpu.VMEM(delay.shape, I32),
             pltpu.VMEM(frac.shape, I32),
             pltpu.VMEM(traces.shape, BF16),
-            pltpu.SemaphoreType.DMA((4,)),
+            pltpu.SemaphoreType.DMA((4 + PIECES,)),
         ],
-        in_specs=[SMEM] + [ANY] * 4,
+        in_specs=[SMEM] + [ANY] * 5,
     )
 
     def receivers(far):
@@ -341,13 +360,11 @@
     tables = [jnp.transpose(v[:, 0], (0, 2, 1)) for v in (src_delay, src_frac)]
     source_tables = call(
         functools.partial(source_tables_kernel, peers, share, calls),
-        (stay(src_taper), *tables),
+        (source_taper, *tables),
         (
             shape((peers, peers, per_peer, LANES), I32),
             shape((len(calls), peers, 4 * per_peer, len(calls[0]) * share * per_peer), BF16),
         ),
-        [pltpu.SMEM(src_taper.shape, F32), pltpu.SemaphoreType.DMA],
-        in_specs=[ANY, VMEM, VMEM],
     )
     arrived = near_in + far_in
     result = None

time: 23.9 us -> 23.9 us (level)
  waiting for transfers between devices: 1.48 us -> 1.13 us
  Pallas kernels: 8.84 us -> 9.12 us
    ppermute x7, waiting for transfers between devices: 1.48 us -> 1.13 us  [swap(): return lax.ppermute(block, 'shot', [(i, i ^ step) for i in range(peers)])]
    pallas_call x6 -> x7, Pallas kernels: 8.84 us -> 9.12 us  [call(): pl.pallas_call(kernel, out_shape=outs, in_specs=in_specs or [VMEM] * len(...]
  transfers between devices with their start and end apart: 8 -> 8, of which waited for: 1 -> 2; matrix products, arithmetic and copies ran while one was open for 0% -> 0% of each run, Pallas kernels for 22% -> 25%
where the time goes in v3:
time: 23.9 us; the launch traced here: 23.7 us
  starting transfers between devices  12.7 us (53%)
  Pallas kernels  9.12 us (38%)
  waiting for transfers between devices  1.13 us (5%)
  between operations  0.73 us (3%)
    ppermute x7, starting transfers between devices, swap(): return lax.ppermute(block, 'shot', [(i, i ^ step) for i in range(peers)])  12.2 us
    pallas_call x7, Pallas kernels, call(): pl.pallas_call(kernel, out_shape=outs, in_specs=in_specs or [VMEM] * len(...  9.12 us
    ppermute x7, waiting for transfers between devices, swap(): return lax.ppermute(block, 'shot', [(i, i ^ step) for i in range(peers)])  1.13 us
    ppermute x1, starting transfers between devices, body(): other = lax.ppermute(traces, 'rcv', [(0, 1), (1, 0)])  0.49 us
  transfers between devices with their start and end apart: 8, of which 2 were waited for; matrix products, arithmetic and copies ran while one was open for 0% of the time, Pallas kernels for 25%

profile of v3, /device:TPU:0, one launch (start us, length us, event | category | flops | bytes accessed | tf_op | source)
XLA Modules:
  0.0 23.7 jit_solution(3357043664410506147)
XLA Ops:
  0.0 0.5 %collective-permute-start = (bf16[128,1536]{1,0:T(8,128)(2,1)}, bf16[128,1536]{1,0:T(8,128)(2,1)S(1)}, u32[]{:S(2)}, u32[]{:S(2)}) collective-permute-start(bf16[128,1536]{1,0:T(8,128)(2,1)} %bitcast.32), channel_id=1, source_target_pairs={{0,1},{1,0},{2,3},{3,2},{4,5},{5,4},{6,7},{7,6},{8,9},{9,8},{10,11... | collective-permute-start | bytes 1179656 | tf_op jit(solution)/shard_map/ppermute | solution.py:315
  1.1 1.6 %shard_map.82 = (s32[9,128,128]{2,1,0:T(8,128)S(1)}, f32[4,128,128]{2,1,0:T(8,128)S(1)}, f32[12,128,128]{2,1,0:T(8,128)S(1)}, bf16[512,256]{1,0:T(8,128)(2,1)S(1)}, f32[8,128]{1,0:T(8,128)S(1)}) custom-call(s32[1]{0:T(128)S(6)} %copy.19.live_ref, f32[9]{0:T(128)} %taper_in.1, f32[9]{0:T(128)} %source_taper_in.1, s32[9,1,128]{2,1,0:T(1,128)} %bitcast.34, ...), custom_call_target="tpu_custom_call" | custom-call | tf_op jit(solution)/shard_map/pallas_call | solution.py:298
  2.7 0.0 collective-permute-done.other_ref
  2.8 1.5 %shard_map.85 = bf16[4,16,1536]{2,1,0:T(8,128)(2,1)S(1)} custom-call(bf16[128,1536]{1,0:T(8,128)(2,1)S(1)} %collective-permute-done.other_ref, s32[9,128,128]{2,1,0:T(8,128)S(1)} %get-tuple-element.16.place_ref, f32[4,128,128]{2,1,0:T(8,128)S(1)} %get-tuple-element.17.weight_ref, f32[12,128,128]{2,1,0:T(8,128)S(1)} %get-tuple-element.18.filt_ref, ...), custom_call_target="tpu_custom_call" | custom-call | tf_op jit(solution)/shard_map/pallas_call | solution.py:298
  4.2 0.0 copy-start
  4.2 0.0 copy-start.1
  4.3 4.6 %collective-permute-start.7 = (bf16[16,1536]{1,0:T(8,128)(2,1)S(1)}, bf16[16,1536]{1,0:T(8,128)(2,1)S(1)}, u32[]{:S(2)}, u32[]{:S(2)}) collective-permute-start(bf16[16,1536]{1,0:T(8,128)(2,1)S(1)} %get-tuple-element.19), channel_id=1, source_target_pairs={{0,10},{2,8},{4,14},{6,12},{8,2},{10,0},{12,6},{14,4},{1,11},{3,9}... | collective-permute-start | bytes 147464 | tf_op jit(solution)/shard_map/ppermute | solution.py:389
  8.9 0.3 %collective-permute-start.6 = (bf16[16,1536]{1,0:T(8,128)(2,1)S(1)}, bf16[16,1536]{1,0:T(8,128)(2,1)S(1)}, u32[]{:S(2)}, u32[]{:S(2)}) collective-permute-start(bf16[16,1536]{1,0:T(8,128)(2,1)S(1)} %get-tuple-element.20), channel_id=1, source_target_pairs={{0,8},{2,10},{4,12},{6,14},{8,0},{10,2},{12,4},{14,6},{1,9},{3,11}... | collective-permute-start | bytes 147464 | tf_op jit(solution)/shard_map/ppermute | solution.py:389
  9.2 1.5 %shard_map.84 = bf16[4,16,1536]{2,1,0:T(8,128)(2,1)S(1)} custom-call(bf16[128,1536]{1,0:T(8,128)(2,1)S(1)} %collective-permute-done.other_ref, s32[9,128,128]{2,1,0:T(8,128)S(1)} %get-tuple-element.16.place_ref, f32[4,128,128]{2,1,0:T(8,128)S(1)} %get-tuple-element.17.weight_ref, f32[12,128,128]{2,1,0:T(8,128)S(1)} %get-tuple-element.18.filt_ref, ...), custom_call_target="tpu_custom_call" | custom-call | tf_op jit(solution)/shard_map/pallas_call | solution.py:298
  10.7 3.6 %collective-permute-start.4 = (bf16[16,1536]{1,0:T(8,128)(2,1)S(1)}, bf16[16,1536]{1,0:T(8,128)(2,1)S(1)}, u32[]{:S(2)}, u32[]{:S(2)}) collective-permute-start(bf16[16,1536]{1,0:T(8,128)(2,1)S(1)} %get-tuple-element.21), channel_id=1, source_target_pairs={{0,14},{2,12},{4,10},{6,8},{8,6},{10,4},{12,2},{14,0},{1,15},{3,13... | collective-permute-start | bytes 147464 | tf_op jit(solution)/shard_map/ppermute | solution.py:389
  14.3 0.1 collective-permute-start.3
  14.4 1.6 %collective-permute-start.5 = (bf16[16,1536]{1,0:T(8,128)(2,1)S(1)}, bf16[16,1536]{1,0:T(8,128)(2,1)S(1)}, u32[]{:S(2)}, u32[]{:S(2)}) collective-permute-start(bf16[16,1536]{1,0:T(8,128)(2,1)S(1)} %get-tuple-element.23), channel_id=1, source_target_pairs={{0,2},{2,0},{4,6},{6,4},{8,10},{10,8},{12,14},{14,12},{1,3},{3,1},... | collective-permute-start | bytes 147464 | tf_op jit(solution)/shard_map/ppermute | solution.py:389
  16.0 0.0 collective-permute-done.7.refs_3_
  16.0 0.0 collective-permute-start.2
  16.1 0.0 collective-permute-done.6.refs_2_
  16.1 1.9 %collective-permute-start.1 = (bf16[16,1536]{1,0:T(8,128)(2,1)S(1)}, bf16[16,1536]{1,0:T(8,128)(2,1)S(1)}, u32[]{:S(2)}, u32[]{:S(2)}) collective-permute-start(bf16[16,1536]{1,0:T(8,128)(2,1)S(1)} %get-tuple-element.26), channel_id=1, source_target_pairs={{0,6},{2,4},{4,2},{6,0},{8,14},{10,12},{12,10},{14,8},{1,7},{3,5},... | collective-permute-start | bytes 147464 | tf_op jit(solution)/shard_map/ppermute | solution.py:389
  17.9 0.0 copy-done
  17.9 0.0 copy-done.1
  18.0 0.4 %shard_map.83 = (s32[8,8,16,128]{3,2,1,0:T(8,128)S(1)}, bf16[3,8,64,64]{3,2,1,0:T(8,128)(2,1)S(1)}) custom-call(f32[8,128]{1,0:T(8,128)S(1)} %get-tuple-element.12.taper_ref, s32[8,9,16]{2,1,0:T(8,128)S(1)} %get-tuple-element.28.delay_ref, s32[8,9,16]{2,1,0:T(8,128)S(1)} %get-tuple-element.27.frac_ref), custom_call_target="tpu_custom_call" | custom-call | tf_op jit(solution)/shard_map/pallas_call | solution.py:298
  18.4 0.1 collective-permute-done.5.refs_1_
  18.5 1.2 %shard_map.86.refs_3_ = f32[2,8,16,1536]{3,2,1,0:T(8,128)S(1)} custom-call(s32[8,8,16,128]{3,2,1,0:T(8,128)S(1)} %get-tuple-element.13.place_ref, bf16[3,8,64,64]{3,2,1,0:T(8,128)(2,1)S(1)} %get-tuple-element.14.weight_ref, bf16[512,256]{1,0:T(8,128)(2,1)S(1)} %get-tuple-element.15.band_ref, bf16[16,1536]{1,0:T(8,128)(2,1)S(1)} %get-tuple-element.24.refs_0_, ...), custom_call_target="tpu_custom_call" | custom-call | tf_op jit(solution)/shard_map/pallas_call | solution.py:298
  19.8 0.0 collective-permute-done.4.refs_2_
  19.8 1.0 %collective-permute-done.3.refs_1_ = bf16[16,1536]{1,0:T(8,128)(2,1)S(1)} collective-permute-done((bf16[16,1536]{1,0:T(8,128)(2,1)S(1)}, bf16[16,1536]{1,0:T(8,128)(2,1)S(1)}, u32[]{:S(2)}, u32[]{:S(2)}) %collective-permute-start.3) | collective-permute-done | bytes 49184 | tf_op jit(solution)/shard_map/ppermute | solution.py:389
  20.8 0.0 collective-permute-done.2.refs_0_
  20.8 1.1 %shard_map.87.refs_1_ = f32[2,8,16,1536]{3,2,1,0:T(8,128)S(1)} custom-call(s32[8,8,16,128]{3,2,1,0:T(8,128)S(1)} %get-tuple-element.13.place_ref, bf16[3,8,64,64]{3,2,1,0:T(8,128)(2,1)S(1)} %get-tuple-element.14.weight_ref, bf16[512,256]{1,0:T(8,128)(2,1)S(1)} %get-tuple-element.15.band_ref, bf16[16,1536]{1,0:T(8,128)(2,1)S(1)} %collective-permute-done.2.refs_0_, ...), custom_call_target="tpu_custom_call" | custom-call | tf_op jit(solution)/shard_map/pallas_call | solution.py:298
  21.9 0.0 collective-permute-done.1.refs_0_
  21.9 1.8 %shard_map.88 = bf16[8,16,1536]{2,1,0:T(8,128)(2,1)} custom-call(s32[8,8,16,128]{3,2,1,0:T(8,128)S(1)} %get-tuple-element.13.place_ref, bf16[3,8,64,64]{3,2,1,0:T(8,128)(2,1)S(1)} %get-tuple-element.14.weight_ref, bf16[512,256]{1,0:T(8,128)(2,1)S(1)} %get-tuple-element.15.band_ref, bf16[16,1536]{1,0:T(8,128)(2,1)S(1)} %collective-permute-done.1.refs_0_, ...), custom_call_target="tpu_custom_call" | custom-call | tf_op jit(solution)/shard_map/pallas_call | solution.py:298
  (3 shorter events, 0.0 us)
Async XLA Ops:
  0.0 2.7 %collective-permute-start = (bf16[128,1536]{1,0:T(8,128)(2,1)}, bf16[128,1536]{1,0:T(8,128)(2,1)S(1)}, u32[]{:S(2)}, u32[]{:S(2)}) collective-permute-start(bf16[128,1536]{1,0:T(8,128)(2,1)} %bitcast.32), channel_id=1, source_target_pairs={{0,1},{1,0},{2,3},{3,2},{4,5},{5,4},{6,7},{7,6},{8,9},{9,8},{10,11... | collective-permute-start | bytes 1179656 | tf_op jit(solution)/shard_map/ppermute | solution.py:315
  4.2 13.7 %copy-start = (s32[8,1,16,9]{2,1,3,0:T(1,128)S(1)}, s32[8,1,16,9]{2,1,3,0:T(1,128)}, u32[]{:S(2)}) copy-start(s32[8,1,16,9]{2,1,3,0:T(1,128)} %param.13) | copy-start | bytes 13828
  4.2 13.7 %copy-start.1 = (s32[8,1,16,9]{2,1,3,0:T(1,128)S(1)}, s32[8,1,16,9]{2,1,3,0:T(1,128)}, u32[]{:S(2)}) copy-start(s32[8,1,16,9]{2,1,3,0:T(1,128)} %param.12) | copy-start | bytes 13828
  4.3 11.8 %collective-permute-start.7 = (bf16[16,1536]{1,0:T(8,128)(2,1)S(1)}, bf16[16,1536]{1,0:T(8,128)(2,1)S(1)}, u32[]{:S(2)}, u32[]{:S(2)}) collective-permute-start(bf16[16,1536]{1,0:T(8,128)(2,1)S(1)} %get-tuple-element.19), channel_id=1, source_target_pairs={{0,10},{2,8},{4,14},{6,12},{8,2},{10,0},{12,6},{14,4},{1,11},{3,9}... | collective-permute-start | bytes 147464 | tf_op jit(solution)/shard_map/ppermute | solution.py:389
  8.9 7.2 %collective-permute-start.6 = (bf16[16,1536]{1,0:T(8,128)(2,1)S(1)}, bf16[16,1536]{1,0:T(8,128)(2,1)S(1)}, u32[]{:S(2)}, u32[]{:S(2)}) collective-permute-start(bf16[16,1536]{1,0:T(8,128)(2,1)S(1)} %get-tuple-element.20), channel_id=1, source_target_pairs={{0,8},{2,10},{4,12},{6,14},{8,0},{10,2},{12,4},{14,6},{1,9},{3,11}... | collective-permute-start | bytes 147464 | tf_op jit(solution)/shard_map/ppermute | solution.py:389
  10.7 9.1 %collective-permute-start.4 = (bf16[16,1536]{1,0:T(8,128)(2,1)S(1)}, bf16[16,1536]{1,0:T(8,128)(2,1)S(1)}, u32[]{:S(2)}, u32[]{:S(2)}) collective-permute-start(bf16[16,1536]{1,0:T(8,128)(2,1)S(1)} %get-tuple-element.21), channel_id=1, source_target_pairs={{0,14},{2,12},{4,10},{6,8},{8,6},{10,4},{12,2},{14,0},{1,15},{3,13... | collective-permute-start | bytes 147464 | tf_op jit(solution)/shard_map/ppermute | solution.py:389
  14.3 6.5 %collective-permute-start.3 = (bf16[16,1536]{1,0:T(8,128)(2,1)S(1)}, bf16[16,1536]{1,0:T(8,128)(2,1)S(1)}, u32[]{:S(2)}, u32[]{:S(2)}) collective-permute-start(bf16[16,1536]{1,0:T(8,128)(2,1)S(1)} %get-tuple-element.22), channel_id=1, source_target_pairs={{0,12},{2,14},{4,8},{6,10},{8,4},{10,6},{12,0},{14,2},{1,13},{3,15... | collective-permute-start | bytes 147464 | tf_op jit(solution)/shard_map/ppermute | solution.py:389
  14.4 4.1 %collective-permute-start.5 = (bf16[16,1536]{1,0:T(8,128)(2,1)S(1)}, bf16[16,1536]{1,0:T(8,128)(2,1)S(1)}, u32[]{:S(2)}, u32[]{:S(2)}) collective-permute-start(bf16[16,1536]{1,0:T(8,128)(2,1)S(1)} %get-tuple-element.23), channel_id=1, source_target_pairs={{0,2},{2,0},{4,6},{6,4},{8,10},{10,8},{12,14},{14,12},{1,3},{3,1},... | collective-permute-start | bytes 147464 | tf_op jit(solution)/shard_map/ppermute | solution.py:389
  16.0 4.7 %collective-permute-start.2 = (bf16[16,1536]{1,0:T(8,128)(2,1)S(1)}, bf16[16,1536]{1,0:T(8,128)(2,1)S(1)}, u32[]{:S(2)}, u32[]{:S(2)}) collective-permute-start(bf16[16,1536]{1,0:T(8,128)(2,1)S(1)} %get-tuple-element.25), channel_id=1, source_target_pairs={{0,4},{2,6},{4,0},{6,2},{8,12},{10,14},{12,8},{14,10},{1,5},{3,7},... | collective-permute-start | bytes 147464 | tf_op jit(solution)/shard_map/ppermute | solution.py:389
  16.1 5.8 %collective-permute-start.1 = (bf16[16,1536]{1,0:T(8,128)(2,1)S(1)}, bf16[16,1536]{1,0:T(8,128)(2,1)S(1)}, u32[]{:S(2)}, u32[]{:S(2)}) collective-permute-start(bf16[16,1536]{1,0:T(8,128)(2,1)S(1)} %get-tuple-element.26), channel_id=1, source_target_pairs={{0,6},{2,4},{4,2},{6,0},{8,14},{10,12},{12,10},{14,8},{1,7},{3,5},... | collective-permute-start | bytes 147464 | tf_op jit(solution)/shard_map/ppermute | solution.py:389

commit v4 on v3

--- a/solution.py
+++ b/solution.py
@@ -100,6 +100,18 @@
             first.append(dot[:rows, cols] + dot[rows : 2 * rows, cols])
             second.append(dot[2 * rows : 3 * rows, cols] + dot[3 * rows :, cols])
     return first, second
+
+
+def products(weights, taps, blocks, rows):
+    values = []
+    step = pair_of(blocks)
+    for b in range(0, blocks, step):
+        stack = jnp.concatenate(
+            [jnp.concatenate([tap[b + i] for tap in taps], axis=0).astype(BF16) for i in range(step)], axis=1
+        )
+        dot = jnp.dot(weights, stack, preferred_element_type=F32)
+        values += [dot[:rows, i * LANES : (i + 1) * LANES] + dot[rows:, i * LANES : (i + 1) * LANES] for i in range(step)]
+    return values
 
 
 def join(first, second):
@@ -261,22 +273,33 @@
     rows = min(SUB, per_peer)
     copies = []
     for k in range(peers):
-        taps = []
+        taps, ahead = [], []
         for i in range(used):
             for r in range(0, per_peer, rows):
                 at = slice(r, r + rows)
-                taps.append(shifted(lambda b: src_ref[i, b, at, :], place_ref[k, shots[i], at, :], blocks))
-        pair = sums(weight_ref[turn, k, :, : used * per_peer], taps, blocks, per_peer)
+                place = place_ref[k, shots[i], at, :]
+                taps.append(shifted(lambda b: src_ref[i, b, at, :], place, blocks))
+                if last:
+                    ahead.append(shifted(lambda b: src_ref[i, b, at, :], place + 1, blocks))
+        weights = weight_ref[turn, k, :, : used * per_peer]
+        if last:
+            half = 2 * per_peer
+            here = products(weights[:half], taps, blocks, per_peer)
+            there = products(weights[half:], ahead, blocks, per_peer)
+            for b in range(blocks):
+                cols = slice(b * LANES, (b + 1) * LANES)
+                done_ref[k, :, cols] = (here[b] + there[b] + part_ref[k, :, cols]).astype(BF16)
+            copies.append(pltpu.make_async_copy(done_ref.at[k], out_ref.at[k], sem.at[k]))
+            copies[-1].start()
+            continue
+        pair = sums(weights, taps, blocks, per_peer)
         if turn:
             pair = [
                 [v + part_ref[i, k, :, b * LANES : (b + 1) * LANES] for b, v in enumerate(part)]
                 for i, part in enumerate(pair)
             ]
-        if last:
             for b, value in enumerate(join(*pair)):
-                done_ref[k, :, b * LANES : (b + 1) * LANES] = value.astype(BF16)
-            copies.append(pltpu.make_async_copy(done_ref.at[k], out_ref.at[k], sem.at[k]))
-            copies[-1].start()
+                out_ref[k, :, b * LANES : (b + 1) * LANES] = value
         else:
             for i, part in enumerate(pair):
                 for b, value in enumerate(part):
@@ -378,7 +401,7 @@
         result = call(
             functools.partial(source_kernel, turn, last, peers, share, groups),
             (*source_tables, band, *ins, *extra),
-            shape((peers, per_peer, time), BF16) if last else shape((2, peers, per_peer, time), F32),
+            shape((peers, per_peer, time), BF16 if last else F32) if turn else shape((2, peers, per_peer, time), F32),
             scratch,
             out_specs=ANY if last else VMEM,
         )

time: 23.9 us -> 23.8 us (level)
  no operation moved by 1% of the time
where the time goes in v4:
time: 23.8 us; the launch traced here: 23.7 us
  starting transfers between devices  12.7 us (53%)
  Pallas kernels  9.09 us (38%)
  waiting for transfers between devices  1.13 us (5%)
  between operations  0.73 us (3%)
    ppermute x7, starting transfers between devices, swap(): return lax.ppermute(block, 'shot', [(i, i ^ step) for i in range(peers)])  12.2 us
    pallas_call x7, Pallas kernels, call(): pl.pallas_call(kernel, out_shape=outs, in_specs=in_specs or [VMEM] * len(...  9.09 us
    ppermute x7, waiting for transfers between devices, swap(): return lax.ppermute(block, 'shot', [(i, i ^ step) for i in range(peers)])  1.13 us
    ppermute x1, starting transfers between devices, body(): other = lax.ppermute(traces, 'rcv', [(0, 1), (1, 0)])  0.49 us
  transfers between devices with their start and end apart: 8, of which 2 were waited for; matrix products, arithmetic and copies ran while one was open for 0% of the time, Pallas kernels for 25%

profile of v4, /device:TPU:0, one launch (start us, length us, event | category | flops | bytes accessed | tf_op | source)
XLA Modules:
  0.0 23.7 jit_solution(16265423562110974874)
XLA Ops:
  0.0 0.5 %collective-permute-start = (bf16[128,1536]{1,0:T(8,128)(2,1)}, bf16[128,1536]{1,0:T(8,128)(2,1)S(1)}, u32[]{:S(2)}, u32[]{:S(2)}) collective-permute-start(bf16[128,1536]{1,0:T(8,128)(2,1)} %bitcast.32), channel_id=1, source_target_pairs={{0,1},{1,0},{2,3},{3,2},{4,5},{5,4},{6,7},{7,6},{8,9},{9,8},{10,11... | collective-permute-start | bytes 1179656 | tf_op jit(solution)/shard_map/ppermute | solution.py:338
  1.1 1.6 %shard_map.82 = (s32[9,128,128]{2,1,0:T(8,128)S(1)}, f32[4,128,128]{2,1,0:T(8,128)S(1)}, f32[12,128,128]{2,1,0:T(8,128)S(1)}, bf16[512,256]{1,0:T(8,128)(2,1)S(1)}, f32[8,128]{1,0:T(8,128)S(1)}) custom-call(s32[1]{0:T(128)S(6)} %copy.19.live_ref, f32[9]{0:T(128)} %taper_in.1, f32[9]{0:T(128)} %source_taper_in.1, s32[9,1,128]{2,1,0:T(1,128)} %bitcast.34, ...), custom_call_target="tpu_custom_call" | custom-call | tf_op jit(solution)/shard_map/pallas_call | solution.py:321
  2.7 0.0 collective-permute-done.other_ref
  2.8 1.5 %shard_map.85 = bf16[4,16,1536]{2,1,0:T(8,128)(2,1)S(1)} custom-call(bf16[128,1536]{1,0:T(8,128)(2,1)S(1)} %collective-permute-done.other_ref, s32[9,128,128]{2,1,0:T(8,128)S(1)} %get-tuple-element.16.place_ref, f32[4,128,128]{2,1,0:T(8,128)S(1)} %get-tuple-element.17.weight_ref, f32[12,128,128]{2,1,0:T(8,128)S(1)} %get-tuple-element.18.filt_ref, ...), custom_call_target="tpu_custom_call" | custom-call | tf_op jit(solution)/shard_map/pallas_call | solution.py:321
  4.2 0.0 copy-start
  4.2 0.0 copy-start.1
  4.3 4.6 %collective-permute-start.7 = (bf16[16,1536]{1,0:T(8,128)(2,1)S(1)}, bf16[16,1536]{1,0:T(8,128)(2,1)S(1)}, u32[]{:S(2)}, u32[]{:S(2)}) collective-permute-start(bf16[16,1536]{1,0:T(8,128)(2,1)S(1)} %get-tuple-element.19), channel_id=1, source_target_pairs={{0,10},{2,8},{4,14},{6,12},{8,2},{10,0},{12,6},{14,4},{1,11},{3,9}... | collective-permute-start | bytes 147464 | tf_op jit(solution)/shard_map/ppermute | solution.py:412
  8.9 0.3 %collective-permute-start.6 = (bf16[16,1536]{1,0:T(8,128)(2,1)S(1)}, bf16[16,1536]{1,0:T(8,128)(2,1)S(1)}, u32[]{:S(2)}, u32[]{:S(2)}) collective-permute-start(bf16[16,1536]{1,0:T(8,128)(2,1)S(1)} %get-tuple-element.20), channel_id=1, source_target_pairs={{0,8},{2,10},{4,12},{6,14},{8,0},{10,2},{12,4},{14,6},{1,9},{3,11}... | collective-permute-start | bytes 147464 | tf_op jit(solution)/shard_map/ppermute | solution.py:412
  9.2 1.5 %shard_map.84 = bf16[4,16,1536]{2,1,0:T(8,128)(2,1)S(1)} custom-call(bf16[128,1536]{1,0:T(8,128)(2,1)S(1)} %collective-permute-done.other_ref, s32[9,128,128]{2,1,0:T(8,128)S(1)} %get-tuple-element.16.place_ref, f32[4,128,128]{2,1,0:T(8,128)S(1)} %get-tuple-element.17.weight_ref, f32[12,128,128]{2,1,0:T(8,128)S(1)} %get-tuple-element.18.filt_ref, ...), custom_call_target="tpu_custom_call" | custom-call | tf_op jit(solution)/shard_map/pallas_call | solution.py:321
  10.7 3.6 %collective-permute-start.4 = (bf16[16,1536]{1,0:T(8,128)(2,1)S(1)}, bf16[16,1536]{1,0:T(8,128)(2,1)S(1)}, u32[]{:S(2)}, u32[]{:S(2)}) collective-permute-start(bf16[16,1536]{1,0:T(8,128)(2,1)S(1)} %get-tuple-element.21), channel_id=1, source_target_pairs={{0,14},{2,12},{4,10},{6,8},{8,6},{10,4},{12,2},{14,0},{1,15},{3,13... | collective-permute-start | bytes 147464 | tf_op jit(solution)/shard_map/ppermute | solution.py:412
  14.3 0.1 collective-permute-start.3
  14.4 1.6 %collective-permute-start.5 = (bf16[16,1536]{1,0:T(8,128)(2,1)S(1)}, bf16[16,1536]{1,0:T(8,128)(2,1)S(1)}, u32[]{:S(2)}, u32[]{:S(2)}) collective-permute-start(bf16[16,1536]{1,0:T(8,128)(2,1)S(1)} %get-tuple-element.23), channel_id=1, source_target_pairs={{0,2},{2,0},{4,6},{6,4},{8,10},{10,8},{12,14},{14,12},{1,3},{3,1},... | collective-permute-start | bytes 147464 | tf_op jit(solution)/shard_map/ppermute | solution.py:412
  16.0 0.0 collective-permute-done.7.refs_3_
  16.0 0.0 collective-permute-start.2
  16.1 0.0 collective-permute-done.6.refs_2_
  16.1 1.9 %collective-permute-start.1 = (bf16[16,1536]{1,0:T(8,128)(2,1)S(1)}, bf16[16,1536]{1,0:T(8,128)(2,1)S(1)}, u32[]{:S(2)}, u32[]{:S(2)}) collective-permute-start(bf16[16,1536]{1,0:T(8,128)(2,1)S(1)} %get-tuple-element.26), channel_id=1, source_target_pairs={{0,6},{2,4},{4,2},{6,0},{8,14},{10,12},{12,10},{14,8},{1,7},{3,5},... | collective-permute-start | bytes 147464 | tf_op jit(solution)/shard_map/ppermute | solution.py:412
  17.9 0.0 copy-done
  17.9 0.0 copy-done.1
  18.0 0.4 %shard_map.83 = (s32[8,8,16,128]{3,2,1,0:T(8,128)S(1)}, bf16[3,8,64,64]{3,2,1,0:T(8,128)(2,1)S(1)}) custom-call(f32[8,128]{1,0:T(8,128)S(1)} %get-tuple-element.12.taper_ref, s32[8,9,16]{2,1,0:T(8,128)S(1)} %get-tuple-element.28.delay_ref, s32[8,9,16]{2,1,0:T(8,128)S(1)} %get-tuple-element.27.frac_ref), custom_call_target="tpu_custom_call" | custom-call | tf_op jit(solution)/shard_map/pallas_call | solution.py:321
  18.4 0.1 collective-permute-done.5.refs_1_
  18.5 1.2 %shard_map.86.refs_3_ = f32[2,8,16,1536]{3,2,1,0:T(8,128)S(1)} custom-call(s32[8,8,16,128]{3,2,1,0:T(8,128)S(1)} %get-tuple-element.13.place_ref, bf16[3,8,64,64]{3,2,1,0:T(8,128)(2,1)S(1)} %get-tuple-element.14.weight_ref, bf16[512,256]{1,0:T(8,128)(2,1)S(1)} %get-tuple-element.15.band_ref, bf16[16,1536]{1,0:T(8,128)(2,1)S(1)} %get-tuple-element.24.refs_0_, ...), custom_call_target="tpu_custom_call" | custom-call | tf_op jit(solution)/shard_map/pallas_call | solution.py:321
  19.8 0.0 collective-permute-done.4.refs_2_
  19.8 1.0 %collective-permute-done.3.refs_1_ = bf16[16,1536]{1,0:T(8,128)(2,1)S(1)} collective-permute-done((bf16[16,1536]{1,0:T(8,128)(2,1)S(1)}, bf16[16,1536]{1,0:T(8,128)(2,1)S(1)}, u32[]{:S(2)}, u32[]{:S(2)}) %collective-permute-start.3) | collective-permute-done | bytes 49184 | tf_op jit(solution)/shard_map/ppermute | solution.py:412
  20.8 0.0 collective-permute-done.2.refs_0_
  20.8 1.2 %shard_map.87.refs_1_ = f32[8,16,1536]{2,1,0:T(8,128)S(1)} custom-call(s32[8,8,16,128]{3,2,1,0:T(8,128)S(1)} %get-tuple-element.13.place_ref, bf16[3,8,64,64]{3,2,1,0:T(8,128)(2,1)S(1)} %get-tuple-element.14.weight_ref, bf16[512,256]{1,0:T(8,128)(2,1)S(1)} %get-tuple-element.15.band_ref, bf16[16,1536]{1,0:T(8,128)(2,1)S(1)} %collective-permute-done.2.refs_0_, ...), custom_call_target="tpu_custom_call" | custom-call | tf_op jit(solution)/shard_map/pallas_call | solution.py:321
  22.0 0.0 collective-permute-done.1.refs_0_
  22.0 1.7 %shard_map.88 = bf16[8,16,1536]{2,1,0:T(8,128)(2,1)} custom-call(s32[8,8,16,128]{3,2,1,0:T(8,128)S(1)} %get-tuple-element.13.place_ref, bf16[3,8,64,64]{3,2,1,0:T(8,128)(2,1)S(1)} %get-tuple-element.14.weight_ref, bf16[512,256]{1,0:T(8,128)(2,1)S(1)} %get-tuple-element.15.band_ref, bf16[16,1536]{1,0:T(8,128)(2,1)S(1)} %collective-permute-done.1.refs_0_, ...), custom_call_target="tpu_custom_call" | custom-call | tf_op jit(solution)/shard_map/pallas_call | solution.py:321
  (3 shorter events, 0.0 us)
Async XLA Ops:
  0.0 2.7 %collective-permute-start = (bf16[128,1536]{1,0:T(8,128)(2,1)}, bf16[128,1536]{1,0:T(8,128)(2,1)S(1)}, u32[]{:S(2)}, u32[]{:S(2)}) collective-permute-start(bf16[128,1536]{1,0:T(8,128)(2,1)} %bitcast.32), channel_id=1, source_target_pairs={{0,1},{1,0},{2,3},{3,2},{4,5},{5,4},{6,7},{7,6},{8,9},{9,8},{10,11... | collective-permute-start | bytes 1179656 | tf_op jit(solution)/shard_map/ppermute | solution.py:338
  4.2 13.7 %copy-start = (s32[8,1,16,9]{2,1,3,0:T(1,128)S(1)}, s32[8,1,16,9]{2,1,3,0:T(1,128)}, u32[]{:S(2)}) copy-start(s32[8,1,16,9]{2,1,3,0:T(1,128)} %param.13) | copy-start | bytes 13828
  4.2 13.7 %copy-start.1 = (s32[8,1,16,9]{2,1,3,0:T(1,128)S(1)}, s32[8,1,16,9]{2,1,3,0:T(1,128)}, u32[]{:S(2)}) copy-start(s32[8,1,16,9]{2,1,3,0:T(1,128)} %param.12) | copy-start | bytes 13828
  4.3 11.8 %collective-permute-start.7 = (bf16[16,1536]{1,0:T(8,128)(2,1)S(1)}, bf16[16,1536]{1,0:T(8,128)(2,1)S(1)}, u32[]{:S(2)}, u32[]{:S(2)}) collective-permute-start(bf16[16,1536]{1,0:T(8,128)(2,1)S(1)} %get-tuple-element.19), channel_id=1, source_target_pairs={{0,10},{2,8},{4,14},{6,12},{8,2},{10,0},{12,6},{14,4},{1,11},{3,9}... | collective-permute-start | bytes 147464 | tf_op jit(solution)/shard_map/ppermute | solution.py:412
  8.9 7.2 %collective-permute-start.6 = (bf16[16,1536]{1,0:T(8,128)(2,1)S(1)}, bf16[16,1536]{1,0:T(8,128)(2,1)S(1)}, u32[]{:S(2)}, u32[]{:S(2)}) collective-permute-start(bf16[16,1536]{1,0:T(8,128)(2,1)S(1)} %get-tuple-element.20), channel_id=1, source_target_pairs={{0,8},{2,10},{4,12},{6,14},{8,0},{10,2},{12,4},{14,6},{1,9},{3,11}... | collective-permute-start | bytes 147464 | tf_op jit(solution)/shard_map/ppermute | solution.py:412
  10.7 9.1 %collective-permute-start.4 = (bf16[16,1536]{1,0:T(8,128)(2,1)S(1)}, bf16[16,1536]{1,0:T(8,128)(2,1)S(1)}, u32[]{:S(2)}, u32[]{:S(2)}) collective-permute-start(bf16[16,1536]{1,0:T(8,128)(2,1)S(1)} %get-tuple-element.21), channel_id=1, source_target_pairs={{0,14},{2,12},{4,10},{6,8},{8,6},{10,4},{12,2},{14,0},{1,15},{3,13... | collective-permute-start | bytes 147464 | tf_op jit(solution)/shard_map/ppermute | solution.py:412
  14.3 6.5 %collective-permute-start.3 = (bf16[16,1536]{1,0:T(8,128)(2,1)S(1)}, bf16[16,1536]{1,0:T(8,128)(2,1)S(1)}, u32[]{:S(2)}, u32[]{:S(2)}) collective-permute-start(bf16[16,1536]{1,0:T(8,128)(2,1)S(1)} %get-tuple-element.22), channel_id=1, source_target_pairs={{0,12},{2,14},{4,8},{6,10},{8,4},{10,6},{12,0},{14,2},{1,13},{3,15... | collective-permute-start | bytes 147464 | tf_op jit(solution)/shard_map/ppermute | solution.py:412
  14.4 4.1 %collective-permute-start.5 = (bf16[16,1536]{1,0:T(8,128)(2,1)S(1)}, bf16[16,1536]{1,0:T(8,128)(2,1)S(1)}, u32[]{:S(2)}, u32[]{:S(2)}) collective-permute-start(bf16[16,1536]{1,0:T(8,128)(2,1)S(1)} %get-tuple-element.23), channel_id=1, source_target_pairs={{0,2},{2,0},{4,6},{6,4},{8,10},{10,8},{12,14},{14,12},{1,3},{3,1},... | collective-permute-start | bytes 147464 | tf_op jit(solution)/shard_map/ppermute | solution.py:412
  16.0 4.7 %collective-permute-start.2 = (bf16[16,1536]{1,0:T(8,128)(2,1)S(1)}, bf16[16,1536]{1,0:T(8,128)(2,1)S(1)}, u32[]{:S(2)}, u32[]{:S(2)}) collective-permute-start(bf16[16,1536]{1,0:T(8,128)(2,1)S(1)} %get-tuple-element.25), channel_id=1, source_target_pairs={{0,4},{2,6},{4,0},{6,2},{8,12},{10,14},{12,8},{14,10},{1,5},{3,7},... | collective-permute-start | bytes 147464 | tf_op jit(solution)/shard_map/ppermute | solution.py:412
  16.1 5.9 %collective-permute-start.1 = (bf16[16,1536]{1,0:T(8,128)(2,1)S(1)}, bf16[16,1536]{1,0:T(8,128)(2,1)S(1)}, u32[]{:S(2)}, u32[]{:S(2)}) collective-permute-start(bf16[16,1536]{1,0:T(8,128)(2,1)S(1)} %get-tuple-element.26), channel_id=1, source_target_pairs={{0,6},{2,4},{4,2},{6,0},{8,14},{10,12},{12,10},{14,8},{1,7},{3,5},... | collective-permute-start | bytes 147464 | tf_op jit(solution)/shard_map/ppermute | solution.py:412
